TPU v7x, 32 devices: a whole 2x2x4 slice. The times are simulated.
32 devices in a mesh: groups: 2 (over x), col: 16 (over z, y, core).
Axes of the slice: x: 2, y: 2, z: 4, core: 2. Of those that a mesh axis runs over, the one named last changes fastest.
Arguments:
- queries: bfloat16 [4096, 896], P(('groups', 'col')), parts along dimension 0, may hold values from -128 to 128
- keys: bfloat16 [4096, 128], P(('groups', 'col')), parts along dimension 0, may hold values from -6 to 6
- values: bfloat16 [4096, 128], P(('groups', 'col')), parts along dimension 0, may hold values from -6 to 6
- out_weight: bfloat16 [896, 3584], replicated, may hold values from -6 to 6
Outputs:
- projected: bfloat16 [4096, 3584], P(('groups', 'col')), parts along dimension 0
There are 2 independent parts, one for each index of `groups`. A program takes and returns all parts, laid end to end along the dimension named above; an argument that names none is the same for every part. Nothing has to cross between parts.
All inputs are finite; a program needn't handle non-finite values.
Results may differ from a plain program's by a relative error of at most 0.0095.
Values may be sent and summed in bfloat16 or wider, within the bound.
No kernel may reach another device: no remote copies, remote signals or barrier semaphores. Data moves between devices by JAX's collectives and lax.ppermute only.
A program may use at most 64 MiB of HBM per device.

v0:
```python
import math

import jax
import jax.numpy as jnp
from jax import lax
from jax.sharding import PartitionSpec as P


def per_device(queries, keys, values, out_weight):
    row_count = queries.shape[0]
    head_size = keys.shape[1]
    head_count = queries.shape[1] // head_size
    factor = head_size ** (-0.5)
    split_queries = queries.reshape(row_count, head_count, head_size)

    def step(carry, pair):
        highest, weight_sum, numerator = carry
        key_block, value_block = pair
        scores = (
            jnp.einsum("thd,sd->hts", split_queries, key_block, preferred_element_type=jnp.float32)
            * factor
        )
        block_max = jnp.max(scores, axis=-1)
        new_max = jnp.maximum(highest, block_max)
        rescale = jnp.exp(highest - new_max)
        expo = jnp.exp(scores - new_max[:, :, None])
        weight_sum = weight_sum * rescale + jnp.sum(expo, axis=-1)
        update = jnp.einsum(
            "hts,sd->thd",
            expo.astype(jnp.bfloat16),
            value_block,
            preferred_element_type=jnp.float32,
        )
        numerator = numerator * jnp.transpose(rescale)[:, :, None] + update
        return ((new_max, weight_sum, numerator), None)

    initial = (
        jnp.full((head_count, row_count), -1e30, jnp.float32),
        jnp.zeros((head_count, row_count), jnp.float32),
        jnp.zeros((row_count, head_count, head_size), jnp.float32),
    )
    gathered_keys, gathered_values = (
        lax.all_gather(keys, "col", axis=0, tiled=True),
        lax.all_gather(values, "col", axis=0, tiled=True),
    )
    rows = gathered_keys.shape[0]
    block = math.gcd(rows, 2048)
    blocks = rows // block
    key_blocks = gathered_keys.reshape(blocks, block, head_size)
    value_blocks = gathered_values.reshape(blocks, block, head_size)
    result, unused = lax.scan(step, initial, (key_blocks, value_blocks))
    highest, weight_sum, numerator = result
    attended = (numerator / jnp.transpose(weight_sum)[:, :, None]).astype(jnp.bfloat16)
    attended = attended.reshape(row_count, head_count * head_size)
    return jnp.dot(attended, out_weight, preferred_element_type=jnp.float32).astype(jnp.bfloat16)


def solution(mesh):
    return jax.shard_map(
        per_device,
        mesh=mesh,
        in_specs=(
            P(("groups", "col"), None),
            P(("groups", "col"), None),
            P(("groups", "col"), None),
            P(),
        ),
        out_specs=P(("groups", "col"), None),
        check_vma=False,
    )
```

profile of v0, /device:TPU:0, one launch (start us, length us, event | category | flops | bytes accessed | tf_op | source)
XLA Modules:
  0.0 57.1 jit_solution(17787351609240946457)
XLA Ops:
  0.0 24.8 %all_gather.6 = bf16[2048,128]{1,0:T(8,128)(2,1)S(1)} all-gather(bf16[128,128]{1,0:T(8,128)(2,1)} %param.5), channel_id=1, replica_groups=mesh['groups'=2,'col'=16] {'col'}, dimensions={0}, use_global_device_ids=true | all-gather | bytes 557056 | tf_op jit(solution)/shard_map/all_gather | solution.py:43
  24.8 1.1 %copy.8 = bf16[128,896]{0,1:T(8,128)(2,1)S(1)} copy(bf16[128,896]{1,0:T(8,128)(2,1)} %param.4) | data formatting | bytes 458752 | tf_op args[0]
  25.9 0.0 copy-start.1
  25.9 1.1 %bitcast_reduce_fusion = (f32[7,128]{1,0:T(8,128)S(1)}, f32[2048,128,7]{1,0,2:T(8,128)S(1)}) fusion(bf16[128,7,128]{0,2,1:T(8,128)(2,1)S(1)} %bitcast.47, bf16[2048,128]{1,0:T(8,128)(2,1)S(1)} %all_gather.6), kind=kOutput, calls=%fused_computation.1 | convolution fusion | flops 473431168 | bytes 8097280 | tf_op jit(solution)/shard_map/while/body/eval_jaxpr/thd,sd->hts/dot_general | solution.py:20
  27.0 0.0 copy-start
  27.1 2.9 %copy-done = f32[2048,128,7]{1,0,2:T(8,128)} copy-done((f32[2048,128,7]{1,0,2:T(8,128)}, f32[2048,128,7]{1,0,2:T(8,128)S(1)}, u32[]{:S(2)}) %copy-start) | copy-done | bytes 7340056
  30.0 0.0 slice-start
  30.0 1.2 %fusion.1 = f32[7,128]{1,0:T(8,128)S(1)} fusion(f32[2048,128,7]{1,0,2:T(8,128)S(1)} %get-tuple-element.20, f32[7,128]{1,0:T(8,128)S(1)} %get-tuple-element.18), kind=kLoop, calls=%fused_computation.3 | loop fusion | flops 5504128 | bytes 7347200 | tf_op jit(solution)/shard_map/while/body/eval_jaxpr/reduce_sum | solution.py:27
  31.2 0.0 copy-done.1
  31.2 0.1 copy.10
  31.3 18.9 %all_gather.7 = bf16[2048,128]{0,1:T(8,128)(2,1)S(1)} all-gather(bf16[128,128]{0,1:T(8,128)(2,1)S(1)} %copy.10), channel_id=1, replica_groups=mesh['groups'=2,'col'=16] {'col'}, dimensions={0}, use_global_device_ids=true | all-gather | bytes 557056 | tf_op jit(solution)/shard_map/all_gather | solution.py:44
  50.2 0.0 slice-start.1
  50.2 4.7 %fusion.14 = bf16[128,7,128]{0,2,1:T(8,128)(2,1)S(1)} fusion(f32[2048,128,7]{1,0,2:T(8,128)} %copy-done, f32[7,128]{1,0:T(8,128)S(1)} %get-tuple-element.18, bf16[2048,128]{0,1:T(8,128)(2,1)S(1)} %all_gather.7, f32[128,7]{0,1:T(8,128)S(1)} %bitcast_add_fusion, f32[128,7]{0,1:T(8,128)S(1)} %get-tuple-element.17), kind=kOutput, calls=%fused_computation.10 | convolution fusion | flops 475611136 | bytes 8104448 | tf_op jit(solution)/shard_map/while/body/eval_jaxpr/hts,sd->thd/dot_general | solution.py:28
  55.0 0.0 slice-done
  55.0 0.0 slice-done.1
  55.0 2.1 %convolution_convert_fusion = bf16[128,3584]{1,0:T(8,128)(2,1)} fusion(bf16[128,896]{0,1:T(8,128)(2,1)S(1)} %bitcast.48, bf16[896,3584]{1,0:T(8,128)(2,1)S(1)} %bitcast.46), kind=kOutput, calls=%fused_computation.5 | convolution fusion | flops 822542336 | bytes 7569408 | tf_op jit(solution)/shard_map/dot_general | solution.py:55
  (3 shorter events, 0.0 us)
Async XLA Ops:
  25.9 5.3 %copy-start.1 = (bf16[128,128]{1,0:T(8,128)(2,1)S(1)}, bf16[128,128]{1,0:T(8,128)(2,1)}, u32[]{:S(2)}) copy-start(bf16[128,128]{1,0:T(8,128)(2,1)} %param.6) | copy-start | bytes 98308
  27.0 3.0 %copy-start = (f32[2048,128,7]{1,0,2:T(8,128)}, f32[2048,128,7]{1,0,2:T(8,128)S(1)}, u32[]{:S(2)}) copy-start(f32[2048,128,7]{1,0,2:T(8,128)S(1)} %get-tuple-element.20) | copy-start | bytes 22020100
  30.0 25.0 %slice-start = ((s8[6422528]{0:T(1024)(128)(4,1)}), s8[2228224]{0:T(1024)(128)(4,1)S(1)}, s32[]{:S(2)}) async-start(s8[6422528]{0:T(1024)(128)(4,1)} %bitcast.45), calls=%async_computation | async-start | bytes 4456448
  50.2 4.8 %slice-start.1 = ((s8[6422528]{0:T(1024)(128)(4,1)}), s8[4194304]{0:T(1024)(128)(4,1)S(1)}, s32[]{:S(2)}) async-start(s8[6422528]{0:T(1024)(128)(4,1)} %bitcast.45), calls=%async_computation.1 | async-start | bytes 8388608
where the time goes:
time: 57.2 us; the launch traced here: 57.1 us
  blocking collectives  43.7 us (76%)
  matrix products  7.92 us (14%)
  local copies, waits for them, and re-layouts  4.16 us (7%)
  other arithmetic  1.22 us (2%)
    all_gather x1, blocking collectives, per_device(): lax.all_gather(keys, 'col', axis=0, tiled=True)  24.8 us
    all_gather x1, blocking collectives, per_device(): lax.all_gather(values, 'col', axis=0, tiled=True)  18.9 us
    dot_general x1, matrix products, step(): jnp.einsum('hts,sd->thd', expo.astype(jnp.bfloat16), value_block, preferr...  4.73 us
    unnamed x10, local copies, waits for them, and re-layouts  4.16 us
    dot_general x1, matrix products, per_device(): jnp.dot(attended, out_weight, preferred_element_type=jnp.float32)  2.07 us
    reduce_sum x1, other arithmetic, step(): weight_sum = weight_sum * rescale + jnp.sum(expo, axis=-1)  1.21 us

commit v1 on v0

v1 whole, which is shorter than its diff:
```python
import math

import jax
import jax.numpy as jnp
from jax import lax
from jax.experimental import pallas as pl
from jax.experimental.pallas import tpu as pltpu
from jax.sharding import PartitionSpec as P

LANES = 128
BLOCK = 1024
HOPS = (
    (8, (0,)),
    (4, (0,)),
    (2, (0,)),
    (1, (0,)),
    (4, (8,)),
    (1, (2, 4)),
    (2, (4, 8)),
    (1, (8, 12)),
    (2, (12,)),
    (1, (6, 10)),
    (1, (14,)),
)
GROUPS = ((-1, 3), (0, 1, 2, 4, 5, 7), (6, 9, 8, 10))


def in_vmem(x):
    return pltpu.with_memory_space_constraint(x, pltpu.VMEM)


def softmax_block(query, keys, values, state, scale):
    rows = query.shape[0]
    tiles = keys.shape[0] // LANES
    scores = lax.dot_general(query, keys, (((1,), (1,)), ((), ())), preferred_element_type=jnp.float32)
    parts = [scores[:, i * LANES : (i + 1) * LANES] for i in range(tiles)]
    peak = parts[0]
    for part in parts[1:]:
        peak = jnp.maximum(peak, part)
    top = jnp.broadcast_to(jnp.max(peak, axis=1, keepdims=True), (rows, LANES))
    if state is not None:
        top = jnp.maximum(top, state[0])
    weights = jnp.concatenate(
        [jnp.exp2((part - top) * scale).astype(jnp.bfloat16) for part in parts], axis=1
    )
    sums = jnp.dot(weights, values, preferred_element_type=jnp.float32)
    if state is not None:
        fade = jnp.exp2((state[0] - top) * scale)
        sums = sums + state[1] * jnp.concatenate([fade, fade], axis=1)
    return top, sums


def attend_head(h, query_ref, unit_refs, state, scale):
    head_size = unit_refs[0].shape[1] // 2
    query = query_ref[:, h * head_size : (h + 1) * head_size]
    pieces = [(u, at) for u in unit_refs for at in range(0, u.shape[0], LANES)]
    step = BLOCK // LANES
    for start in range(0, len(pieces), step):
        block = pieces[start : start + step]
        keys = jnp.concatenate([u[at : at + LANES, :head_size] for u, at in block], axis=0)
        values = jnp.concatenate([u[at : at + LANES, head_size:] for u, at in block], axis=0)
        values = jnp.concatenate([values, jnp.ones_like(values)], axis=1)
        state = softmax_block(query, keys, values, state, scale)
    return state


def attend(queries, units, state):
    rows, width = queries.shape
    head_size = units[0].shape[1] // 2
    heads = width // head_size
    scale = head_size ** (-0.5) * math.log2(math.e)

    def kernel(*refs):
        query_ref, refs = refs[0], refs[1:]
        unit_refs, refs = refs[: len(units)], refs[len(units) :]
        top_out, sums_out = refs[-2:]
        for h in range(heads):
            at = slice(h * rows, (h + 1) * rows)
            before = None if state is None else (refs[0][at], refs[1][at])
            top, sums = attend_head(h, query_ref, unit_refs, before, scale)
            top_out[at] = top
            sums_out[at] = sums

    vmem = pl.BlockSpec(memory_space=pltpu.VMEM)
    args = [queries, *units, *(state or ())]
    return pl.pallas_call(
        kernel,
        out_shape=(
            pltpu.VMEM((heads * rows, LANES), jnp.float32),
            pltpu.VMEM((heads * rows, 2 * head_size), jnp.float32),
        ),
        in_specs=[vmem] * len(args),
        out_specs=(vmem, vmem),
        compiler_params=pltpu.CompilerParams(vmem_limit_bytes=16 << 20),
    )(*[in_vmem(x) for x in args])


def finish(queries, units, state, out_weight):
    rows, width = queries.shape
    head_size = units[0].shape[1] // 2
    heads = width // head_size
    scale = head_size ** (-0.5) * math.log2(math.e)
    columns = out_weight.shape[1]
    strip = math.gcd(columns, 512)
    strips = columns // strip

    def kernel(*refs):
        query_ref, refs = refs[0], refs[1:]
        unit_refs, refs = refs[: len(units)], refs[len(units) :]
        weight_ref, out_ref, attended, staged, sems = refs[-5:]
        for h in range(heads):
            at = slice(h * rows, (h + 1) * rows)
            before = None if state is None else (refs[0][at], refs[1][at])
            _, sums = attend_head(h, query_ref, unit_refs, before, scale)
            attended[:, h * head_size : (h + 1) * head_size] = (
                sums[:, :head_size] / sums[:, head_size:]
            ).astype(jnp.bfloat16)
        left = attended[...]
        copies = []
        for j in range(strips):
            at = slice(j * strip, (j + 1) * strip)
            staged[:, at] = jnp.dot(left, weight_ref[:, at], preferred_element_type=jnp.float32).astype(
                jnp.bfloat16
            )
            window = pl.ds(j * strip, strip)
            copy = pltpu.make_async_copy(staged.at[:, window], out_ref.at[:, window], sems.at[j])
            copy.start()
            copies.append(copy)
        for copy in copies:
            copy.wait()

    vmem = pl.BlockSpec(memory_space=pltpu.VMEM)
    args = [queries, *units, *(state or ()), out_weight]
    return pl.pallas_call(
        kernel,
        out_shape=jax.ShapeDtypeStruct((rows, columns), jnp.bfloat16),
        in_specs=[vmem] * len(args),
        out_specs=pl.BlockSpec(memory_space=pl.ANY),
        scratch_shapes=[
            pltpu.VMEM((rows, width), jnp.bfloat16),
            pltpu.VMEM((rows, columns), jnp.bfloat16),
            pltpu.SemaphoreType.DMA((strips,)),
        ],
        compiler_params=pltpu.CompilerParams(vmem_limit_bytes=16 << 20),
    )(*[in_vmem(x) for x in args])


def gather(own, size):
    low = 16
    if size > low:
        along = [[high * low + i for high in range(size // low)] for i in range(low)]
        own = lax.all_gather(own, "col", axis=0, tiled=True, axis_index_groups=along)
    rows = own.shape[0]
    known = {0: (0, own)}
    results = []
    for mask, held in HOPS:
        parts = []
        for m in held:
            at, array = known[m]
            parts.append(array if array.shape[0] == rows else array[at * rows : (at + 1) * rows])
        source = parts[0] if len(parts) == 1 else jnp.concatenate(parts, axis=0)
        got = lax.ppermute(source, "col", [(j, j ^ mask) for j in range(size)])
        for at, m in enumerate(held):
            known[m ^ mask] = (at, got)
        results.append(got)
    return own, results


def solution(mesh):
    size = mesh.shape["col"]

    def per_device(queries, keys, values, out_weight):
        own = jnp.concatenate([keys, values], axis=1)
        if size % 16:
            return finish(queries, [lax.all_gather(own, "col", axis=0, tiled=True)], None, out_weight)
        own, got = gather(own, size)
        units = [[own if i < 0 else got[i] for i in group] for group in GROUPS]
        state = None
        for group in units[:-1]:
            state = attend(queries, group, state)
        return finish(queries, units[-1], state, out_weight)

    spec = P(("groups", "col"), None)
    return jax.shard_map(
        per_device, mesh=mesh, in_specs=(spec, spec, spec, P()), out_specs=spec, check_vma=False
    )
```

time: 57.2 us -> 28.8 us (0.50)
  blocking collectives: 43.7 us -> 0 us
  starting transfers between devices: 0 us -> 11.7 us
  matrix products: 7.92 us -> 0 us
  waiting for transfers between devices: 0 us -> 6.53 us
  Pallas kernels: 0 us -> 4.92 us
  other arithmetic: 1.22 us -> 0.03 us
  local copies, waits for them, and re-layouts: 4.16 us -> 5.29 us
    all_gather x2 -> x0, blocking collectives: 43.7 us -> none  [the longest x1 24.8 us: per_device(): lax.all_gather(keys, 'col', axis=0, tiled=True)]
    ppermute x0 -> x11, starting transfers between devices: none -> 11.7 us  [gather(): got = lax.ppermute(source, 'col', [(j, j ^ mask) for j in range(size)])]
    dot_general x3 -> x0, matrix products: 7.92 us -> none  [the longest x1 4.73 us: step(): jnp.einsum('hts,sd->thd', expo.astype(jnp.bfloat16), value_block, preferr...]
    ppermute x0 -> x11, waiting for transfers between devices: none -> 6.53 us  [gather(): got = lax.ppermute(source, 'col', [(j, j ^ mask) for j in range(size)])]
    pallas_call x0 -> x3, Pallas kernels: none -> 4.92 us  [the longest x1 2.88 us: finish(): pl.pallas_call(kernel, out_shape=jax.ShapeDtypeStruct((rows, columns), jn...]
    reduce_sum x1 -> x0, other arithmetic: 1.21 us -> none  [step(): weight_sum = weight_sum * rescale + jnp.sum(expo, axis=-1)]
    concatenate x0 -> x1, local copies, waits for them, and re-layouts: none -> 0.77 us  [per_device(): own = jnp.concatenate([keys, values], axis=1)]
    unnamed x10 -> x5, local copies, waits for them, and re-layouts: 4.16 us -> 4.52 us
  transfers between devices with their start and end apart: 0 -> 11, of which waited for: 0 -> 4; matrix products, arithmetic and copies ran while one was open for 0% -> 0% of each run, Pallas kernels for 0% -> 7%
where the time goes in v1:
time: 28.8 us; the launch traced here: 28.5 us
  starting transfers between devices  11.7 us (41%)
  waiting for transfers between devices  6.53 us (23%)
  local copies, waits for them, and re-layouts  5.29 us (18%)
  Pallas kernels  4.92 us (17%)
    ppermute x11, starting transfers between devices, gather(): got = lax.ppermute(source, 'col', [(j, j ^ mask) for j in range(size)])  11.7 us
    ppermute x11, waiting for transfers between devices, gather(): got = lax.ppermute(source, 'col', [(j, j ^ mask) for j in range(size)])  6.53 us
    unnamed x5, local copies, waits for them, and re-layouts  4.52 us
    pallas_call x1, Pallas kernels, finish(): pl.pallas_call(kernel, out_shape=jax.ShapeDtypeStruct((rows, columns), jn...  2.88 us
    pallas_call x2, Pallas kernels, attend(): pl.pallas_call(kernel, out_shape=(pltpu.VMEM((heads * rows, LANES), jnp.f...  2.03 us
    concatenate x1, local copies, waits for them, and re-layouts, per_device(): own = jnp.concatenate([keys, values], axis=1)  0.77 us
  transfers between devices with their start and end apart: 11, of which 4 were waited for; matrix products, arithmetic and copies ran while one was open for 0% of the time, Pallas kernels for 7%

profile of v1, /device:TPU:0, one launch (start us, length us, event | category | flops | bytes accessed | tf_op | source)
XLA Modules:
  0.0 28.5 jit_solution(11317964429214727296)
XLA Ops:
  0.0 0.8 %constant_dynamic-update-slice_fusion.1 = bf16[128,256]{1,0:T(8,128)(2,1)S(1)} fusion(bf16[128,128]{1,0:T(8,128)(2,1)} %param.5), kind=kLoop, calls=%fused_computation.4 | loop fusion | bytes 65536
  0.8 0.8 %constant_dynamic-update-slice_fusion.refs_1_ = bf16[128,256]{1,0:T(8,128)(2,1)S(1)} fusion(bf16[128,256]{1,0:T(8,128)(2,1)S(1)} %constant_dynamic-update-slice_fusion.1, bf16[128,128]{1,0:T(8,128)(2,1)} %param.6), kind=kLoop, calls=%fused_computation.3 | loop fusion | bytes 65536 | tf_op jit(solution)/shard_map/concatenate | solution.py:173
  1.5 4.1 %collective-permute-start.1 = (bf16[128,256]{1,0:T(8,128)(2,1)S(1)}, bf16[128,256]{1,0:T(8,128)(2,1)S(1)}, u32[]{:S(2)}, u32[]{:S(2)}) collective-permute-start(bf16[128,256]{1,0:T(8,128)(2,1)S(1)} %constant_dynamic-update-slice_fusion.refs_1_), channel_id=1, source_target_pairs={{0,8},{1,9},{2,10},{3,11},{4,12},{5,13},{6,14},{7,15},{8,0},{9,1},... | collective-permute-start | bytes 196616 | tf_op jit(solution)/shard_map/ppermute | solution.py:162
  5.7 1.6 %collective-permute-start = (bf16[128,256]{1,0:T(8,128)(2,1)S(1)}, bf16[128,256]{1,0:T(8,128)(2,1)S(1)}, u32[]{:S(2)}, u32[]{:S(2)}) collective-permute-start(bf16[128,256]{1,0:T(8,128)(2,1)S(1)} %constant_dynamic-update-slice_fusion.refs_1_), channel_id=1, source_target_pairs={{0,4},{1,5},{2,6},{3,7},{4,0},{5,1},{6,2},{7,3},{8,12},{9,13},{10,... | collective-permute-start | bytes 196616 | tf_op jit(solution)/shard_map/ppermute | solution.py:162
  7.2 1.5 %collective-permute-start.7 = (bf16[128,256]{1,0:T(8,128)(2,1)S(1)}, bf16[128,256]{1,0:T(8,128)(2,1)S(1)}, u32[]{:S(2)}, u32[]{:S(2)}) collective-permute-start(bf16[128,256]{1,0:T(8,128)(2,1)S(1)} %constant_dynamic-update-slice_fusion.refs_1_), channel_id=1, source_target_pairs={{0,2},{1,3},{2,0},{3,1},{4,6},{5,7},{6,4},{7,5},{8,10},{9,11},{10,... | collective-permute-start | bytes 196616 | tf_op jit(solution)/shard_map/ppermute | solution.py:162
  8.8 0.0 collective-permute-done.1.refs_1_
  8.8 1.3 %collective-permute-start.4 = (bf16[128,256]{1,0:T(8,128)(2,1)S(1)}, bf16[128,256]{1,0:T(8,128)(2,1)S(1)}, u32[]{:S(2)}, u32[]{:S(2)}) collective-permute-start(bf16[128,256]{1,0:T(8,128)(2,1)S(1)} %collective-permute-done.1.refs_1_), channel_id=1, source_target_pairs={{0,4},{1,5},{2,6},{3,7},{4,0},{5,1},{6,2},{7,3},{8,12},{9,13},{10,... | collective-permute-start | bytes 196616 | tf_op jit(solution)/shard_map/ppermute | solution.py:162
  10.1 0.0 collective-permute-done.refs_2_
  10.1 1.4 %collective-permute-done.7.refs_3_ = bf16[128,256]{1,0:T(8,128)(2,1)S(1)} collective-permute-done((bf16[128,256]{1,0:T(8,128)(2,1)S(1)}, bf16[128,256]{1,0:T(8,128)(2,1)S(1)}, u32[]{:S(2)}, u32[]{:S(2)}) %collective-permute-start.7) | collective-permute-done | bytes 65568 | tf_op jit(solution)/shard_map/ppermute | solution.py:162
  11.5 1.5 %collective-permute-done.4.refs_4_ = bf16[128,256]{1,0:T(8,128)(2,1)S(1)} collective-permute-done((bf16[128,256]{1,0:T(8,128)(2,1)S(1)}, bf16[128,256]{1,0:T(8,128)(2,1)S(1)}, u32[]{:S(2)}, u32[]{:S(2)}) %collective-permute-start.4) | collective-permute-done | bytes 65568 | tf_op jit(solution)/shard_map/ppermute | solution.py:162
  13.1 1.9 %collective-permute-start.2 = (bf16[256,256]{1,0:T(8,128)(2,1)S(1)}, bf16[256,256]{1,0:T(8,128)(2,1)S(1)}, u32[]{:S(2)}, u32[]{:S(2)}) collective-permute-start(bf16[256,256]{1,0:T(8,128)(2,1)S(1)} %get-tuple-element.14), channel_id=1, source_target_pairs={{0,2},{1,3},{2,0},{3,1},{4,6},{5,7},{6,4},{7,5},{8,10},{9,11},{10,... | collective-permute-start | bytes 393224 | tf_op jit(solution)/shard_map/ppermute | solution.py:162
  15.0 0.0 collective-permute-start.8
  15.0 0.5 %collective-permute-start.9 = (bf16[256,256]{1,0:T(8,128)(2,1)S(1)}, bf16[256,256]{1,0:T(8,128)(2,1)S(1)}, u32[]{:S(2)}, u32[]{:S(2)}) collective-permute-start(bf16[256,256]{1,0:T(8,128)(2,1)S(1)} %get-tuple-element.13), channel_id=1, source_target_pairs={{0,1},{1,0},{2,3},{3,2},{4,5},{5,4},{6,7},{7,6},{8,9},{9,8},{10,11... | collective-permute-start | bytes 393224 | tf_op jit(solution)/shard_map/ppermute | solution.py:162
  15.5 0.2 collective-permute-start.5
  15.7 2.4 %collective-permute-done.2.refs_1_ = bf16[256,256]{1,0:T(8,128)(2,1)S(1)} collective-permute-done((bf16[256,256]{1,0:T(8,128)(2,1)S(1)}, bf16[256,256]{1,0:T(8,128)(2,1)S(1)}, u32[]{:S(2)}, u32[]{:S(2)}) %collective-permute-start.2) | collective-permute-done | bytes 131104 | tf_op jit(solution)/shard_map/ppermute | solution.py:162
  18.1 0.0 collective-permute-start.3
  18.1 0.5 %collective-permute-start.10 = (bf16[128,256]{1,0:T(8,128)(2,1)S(1)}, bf16[128,256]{1,0:T(8,128)(2,1)S(1)}, u32[]{:S(2)}, u32[]{:S(2)}) collective-permute-start(bf16[128,256]{1,0:T(8,128)(2,1)S(1)} %constant_dynamic-update-slice_fusion.refs_1_), channel_id=1, source_target_pairs={{0,1},{1,0},{2,3},{3,2},{4,5},{5,4},{6,7},{7,6},{8,9},{9,8},{10,11... | collective-permute-start | bytes 196616 | tf_op jit(solution)/shard_map/ppermute | solution.py:162
  18.6 1.1 %collective-permute-done.5.refs_3_ = bf16[128,256]{1,0:T(8,128)(2,1)S(1)} collective-permute-done((bf16[128,256]{1,0:T(8,128)(2,1)S(1)}, bf16[128,256]{1,0:T(8,128)(2,1)S(1)}, u32[]{:S(2)}, u32[]{:S(2)}) %collective-permute-start.5) | collective-permute-done | bytes 65568 | tf_op jit(solution)/shard_map/ppermute | solution.py:162
  19.7 0.0 collective-permute-start.6
  19.7 0.0 collective-permute-done.10.refs_2_
  19.7 0.0 copy-start.1
  19.8 0.9 %copy-done.1 = bf16[128,896]{1,0:T(8,128)(2,1)S(1)} copy-done((bf16[128,896]{1,0:T(8,128)(2,1)S(1)}, bf16[128,896]{1,0:T(8,128)(2,1)}, u32[]{:S(2)}) %copy-start.1) | copy-done | bytes 229400
  20.7 0.6 %shard_map.46 = (f32[896,128]{1,0:T(8,128)S(1)}, f32[896,256]{1,0:T(8,128)S(1)}) custom-call(bf16[128,896]{1,0:T(8,128)(2,1)S(1)} %copy-done.1, bf16[128,256]{1,0:T(8,128)(2,1)S(1)} %constant_dynamic-update-slice_fusion.refs_1_, bf16[128,256]{1,0:T(8,128)(2,1)S(1)} %collective-permute-done.10.refs_2_), custom_call_target="tpu_custom_call" | custom-call | tf_op jit(solution)/shard_map/pallas_call | solution.py:86
  21.3 0.0 collective-permute-done.8.refs_5_
  21.3 0.0 collective-permute-done.9.refs_6_
  21.3 1.4 %shard_map.47 = (f32[896,128]{1,0:T(8,128)S(1)}, f32[896,256]{1,0:T(8,128)S(1)}) custom-call(bf16[128,896]{1,0:T(8,128)(2,1)S(1)} %copy-done.1, bf16[128,256]{1,0:T(8,128)(2,1)S(1)} %collective-permute-done.1.refs_1_, bf16[128,256]{1,0:T(8,128)(2,1)S(1)} %collective-permute-done.refs_2_, bf16[128,256]{1,0:T(8,128)(2,1)S(1)} %collective-permute-done.7.refs_3_, ...), custom_call_target="tpu_custom_call" | custom-call | tf_op jit(solution)/shard_map/pallas_call | solution.py:86
  22.8 0.0 collective-permute-done.6.refs_4_
  22.8 0.0 collective-permute-done.3.refs_2_
  22.8 0.0 copy-start
  22.8 2.8 %copy-done = bf16[896,3584]{1,0:T(8,128)(2,1)S(1)} copy-done((bf16[896,3584]{1,0:T(8,128)(2,1)S(1)}, bf16[896,3584]{1,0:T(8,128)(2,1)}, u32[]{:S(2)}) %copy-start) | copy-done | bytes 6422552
  25.6 2.9 %shard_map.48 = bf16[128,3584]{1,0:T(8,128)(2,1)} custom-call(bf16[128,896]{1,0:T(8,128)(2,1)S(1)} %copy-done.1, bf16[256,256]{1,0:T(8,128)(2,1)S(1)} %collective-permute-done.2.refs_1_, bf16[256,256]{1,0:T(8,128)(2,1)S(1)} %collective-permute-done.3.refs_2_, bf16[128,256]{1,0:T(8,128)(2,1)S(1)} %collective-permute-done.5.refs_3_, ...), custom_call_target="tpu_custom_call" | custom-call | tf_op jit(solution)/shard_map/pallas_call | solution.py:134
  (1 shorter events, 0.0 us)
Async XLA Ops:
  1.5 7.2 %collective-permute-start.1 = (bf16[128,256]{1,0:T(8,128)(2,1)S(1)}, bf16[128,256]{1,0:T(8,128)(2,1)S(1)}, u32[]{:S(2)}, u32[]{:S(2)}) collective-permute-start(bf16[128,256]{1,0:T(8,128)(2,1)S(1)} %constant_dynamic-update-slice_fusion.refs_1_), channel_id=1, source_target_pairs={{0,8},{1,9},{2,10},{3,11},{4,12},{5,13},{6,14},{7,15},{8,0},{9,1},... | collective-permute-start | bytes 196616 | tf_op jit(solution)/shard_map/ppermute | solution.py:162
  5.7 4.4 %collective-permute-start = (bf16[128,256]{1,0:T(8,128)(2,1)S(1)}, bf16[128,256]{1,0:T(8,128)(2,1)S(1)}, u32[]{:S(2)}, u32[]{:S(2)}) collective-permute-start(bf16[128,256]{1,0:T(8,128)(2,1)S(1)} %constant_dynamic-update-slice_fusion.refs_1_), channel_id=1, source_target_pairs={{0,4},{1,5},{2,6},{3,7},{4,0},{5,1},{6,2},{7,3},{8,12},{9,13},{10,... | collective-permute-start | bytes 196616 | tf_op jit(solution)/shard_map/ppermute | solution.py:162
  7.2 4.3 %collective-permute-start.7 = (bf16[128,256]{1,0:T(8,128)(2,1)S(1)}, bf16[128,256]{1,0:T(8,128)(2,1)S(1)}, u32[]{:S(2)}, u32[]{:S(2)}) collective-permute-start(bf16[128,256]{1,0:T(8,128)(2,1)S(1)} %constant_dynamic-update-slice_fusion.refs_1_), channel_id=1, source_target_pairs={{0,2},{1,3},{2,0},{3,1},{4,6},{5,7},{6,4},{7,5},{8,10},{9,11},{10,... | collective-permute-start | bytes 196616 | tf_op jit(solution)/shard_map/ppermute | solution.py:162
  8.8 4.3 %collective-permute-start.4 = (bf16[128,256]{1,0:T(8,128)(2,1)S(1)}, bf16[128,256]{1,0:T(8,128)(2,1)S(1)}, u32[]{:S(2)}, u32[]{:S(2)}) collective-permute-start(bf16[128,256]{1,0:T(8,128)(2,1)S(1)} %collective-permute-done.1.refs_1_), channel_id=1, source_target_pairs={{0,4},{1,5},{2,6},{3,7},{4,0},{5,1},{6,2},{7,3},{8,12},{9,13},{10,... | collective-permute-start | bytes 196616 | tf_op jit(solution)/shard_map/ppermute | solution.py:162
  13.1 5.0 %collective-permute-start.2 = (bf16[256,256]{1,0:T(8,128)(2,1)S(1)}, bf16[256,256]{1,0:T(8,128)(2,1)S(1)}, u32[]{:S(2)}, u32[]{:S(2)}) collective-permute-start(bf16[256,256]{1,0:T(8,128)(2,1)S(1)} %get-tuple-element.14), channel_id=1, source_target_pairs={{0,2},{1,3},{2,0},{3,1},{4,6},{5,7},{6,4},{7,5},{8,10},{9,11},{10,... | collective-permute-start | bytes 393224 | tf_op jit(solution)/shard_map/ppermute | solution.py:162
  15.0 6.3 %collective-permute-start.8 = (bf16[256,256]{1,0:T(8,128)(2,1)S(1)}, bf16[256,256]{1,0:T(8,128)(2,1)S(1)}, u32[]{:S(2)}, u32[]{:S(2)}) collective-permute-start(bf16[256,256]{1,0:T(8,128)(2,1)S(1)} %get-tuple-element.15), channel_id=1, source_target_pairs={{0,1},{1,0},{2,3},{3,2},{4,5},{5,4},{6,7},{7,6},{8,9},{9,8},{10,11... | collective-permute-start | bytes 393224 | tf_op jit(solution)/shard_map/ppermute | solution.py:162
  15.0 6.3 %collective-permute-start.9 = (bf16[256,256]{1,0:T(8,128)(2,1)S(1)}, bf16[256,256]{1,0:T(8,128)(2,1)S(1)}, u32[]{:S(2)}, u32[]{:S(2)}) collective-permute-start(bf16[256,256]{1,0:T(8,128)(2,1)S(1)} %get-tuple-element.13), channel_id=1, source_target_pairs={{0,1},{1,0},{2,3},{3,2},{4,5},{5,4},{6,7},{7,6},{8,9},{9,8},{10,11... | collective-permute-start | bytes 393224 | tf_op jit(solution)/shard_map/ppermute | solution.py:162
  15.5 4.3 %collective-permute-start.5 = (bf16[128,256]{1,0:T(8,128)(2,1)S(1)}, bf16[128,256]{1,0:T(8,128)(2,1)S(1)}, u32[]{:S(2)}, u32[]{:S(2)}) collective-permute-start(bf16[128,256]{1,0:T(8,128)(2,1)S(1)} %collective-permute-done.4.refs_4_), channel_id=1, source_target_pairs={{0,2},{1,3},{2,0},{3,1},{4,6},{5,7},{6,4},{7,5},{8,10},{9,11},{10,... | collective-permute-start | bytes 196616 | tf_op jit(solution)/shard_map/ppermute | solution.py:162
  18.1 4.7 %collective-permute-start.3 = (bf16[256,256]{1,0:T(8,128)(2,1)S(1)}, bf16[256,256]{1,0:T(8,128)(2,1)S(1)}, u32[]{:S(2)}, u32[]{:S(2)}) collective-permute-start(bf16[256,256]{1,0:T(8,128)(2,1)S(1)} %collective-permute-done.2.refs_1_), channel_id=1, source_target_pairs={{0,1},{1,0},{2,3},{3,2},{4,5},{5,4},{6,7},{7,6},{8,9},{9,8},{10,11... | collective-permute-start | bytes 393224 | tf_op jit(solution)/shard_map/ppermute | solution.py:162
  18.1 1.6 %collective-permute-start.10 = (bf16[128,256]{1,0:T(8,128)(2,1)S(1)}, bf16[128,256]{1,0:T(8,128)(2,1)S(1)}, u32[]{:S(2)}, u32[]{:S(2)}) collective-permute-start(bf16[128,256]{1,0:T(8,128)(2,1)S(1)} %constant_dynamic-update-slice_fusion.refs_1_), channel_id=1, source_target_pairs={{0,1},{1,0},{2,3},{3,2},{4,5},{5,4},{6,7},{7,6},{8,9},{9,8},{10,11... | collective-permute-start | bytes 196616 | tf_op jit(solution)/shard_map/ppermute | solution.py:162
  19.7 3.0 %collective-permute-start.6 = (bf16[128,256]{1,0:T(8,128)(2,1)S(1)}, bf16[128,256]{1,0:T(8,128)(2,1)S(1)}, u32[]{:S(2)}, u32[]{:S(2)}) collective-permute-start(bf16[128,256]{1,0:T(8,128)(2,1)S(1)} %collective-permute-done.5.refs_3_), channel_id=1, source_target_pairs={{0,1},{1,0},{2,3},{3,2},{4,5},{5,4},{6,7},{7,6},{8,9},{9,8},{10,11... | collective-permute-start | bytes 196616 | tf_op jit(solution)/shard_map/ppermute | solution.py:162
  19.7 0.9 %copy-start.1 = (bf16[128,896]{1,0:T(8,128)(2,1)S(1)}, bf16[128,896]{1,0:T(8,128)(2,1)}, u32[]{:S(2)}) copy-start(bf16[128,896]{1,0:T(8,128)(2,1)} %refs_0_.5) | copy-start | bytes 688132
  22.8 2.8 %copy-start = (bf16[896,3584]{1,0:T(8,128)(2,1)S(1)}, bf16[896,3584]{1,0:T(8,128)(2,1)}, u32[]{:S(2)}) copy-start(bf16[896,3584]{1,0:T(8,128)(2,1)} %refs_7_.1) | copy-start | bytes 19267588

commit v2 on v1

v2 whole, which is shorter than its diff:
```python
import math

import jax
import jax.numpy as jnp
from jax import lax
from jax.experimental import pallas as pl
from jax.experimental.pallas import tpu as pltpu
from jax.sharding import PartitionSpec as P

LANES = 128
BLOCK = 1024
PLAN = (
    ("hop", 8, (0,)),
    ("hop", 4, (0,)),
    ("hop", 2, (0,)),
    ("hop", 1, (0,)),
    ("attend", (0, 1), 2),
    ("hop", 4, (8,)),
    ("hop", 2, (4, 8)),
    ("hop", 1, (2, 4)),
    ("hop", 2, (12,)),
    ("hop", 1, (8, 12)),
    ("attend", (2, 3, 4, 5, 8, 9, 12, 13), 4),
    ("hop", 1, (6, 10)),
    ("hop", 1, (14,)),
)


def in_vmem(x):
    return pltpu.with_memory_space_constraint(x, pltpu.VMEM)


def in_hbm(x):
    return pltpu.with_memory_space_constraint(x, pltpu.HBM)


class Fetch:
    def __init__(self, source, begin, out, sems):
        self.half = out.shape[0] // 2
        self.source, self.begin, self.out, self.sems = source, begin, out, sems

    def copy(self, i):
        at = pl.multiple_of(i * self.half, 16)
        return pltpu.make_async_copy(
            self.source.at[pl.ds(self.begin + at, self.half)], self.out.at[pl.ds(at, self.half)], self.sems.at[i]
        )

    def start(self):
        def one(i, carry):
            self.copy(i).start()
            return carry

        lax.fori_loop(0, 2, one, 0)

    def wait(self):
        for i in range(2):
            self.copy(i).wait()


def softmax_block(query, keys, values, state, scale):
    rows = query.shape[0]
    tiles = keys.shape[0] // LANES
    scores = lax.dot_general(query, keys, (((1,), (1,)), ((), ())), preferred_element_type=jnp.float32)
    parts = [scores[:, i * LANES : (i + 1) * LANES] for i in range(tiles)]
    peak = parts[0]
    for part in parts[1:]:
        peak = jnp.maximum(peak, part)
    top = jnp.broadcast_to(jnp.max(peak, axis=1, keepdims=True), (rows, LANES))
    if state is not None:
        top = jnp.maximum(top, state[0])
    weights = jnp.concatenate(
        [jnp.exp2((part - top) * scale).astype(jnp.bfloat16) for part in parts], axis=1
    )
    sums = jnp.dot(weights, values, preferred_element_type=jnp.float32)
    if state is not None:
        fade = jnp.exp2((state[0] - top) * scale)
        sums = sums + state[1] * jnp.concatenate([fade, fade], axis=1)
    return top, sums


def attend_head(h, query_ref, unit_refs, state, scale):
    head_size = unit_refs[0].shape[1] // 2
    query = query_ref[:, h * head_size : (h + 1) * head_size]
    pieces = [(u, at) for u in unit_refs for at in range(0, u.shape[0], LANES)]
    step = BLOCK // LANES
    for start in range(0, len(pieces), step):
        block = pieces[start : start + step]
        keys = jnp.concatenate([u[at : at + LANES, :head_size] for u, at in block], axis=0)
        values = jnp.concatenate([u[at : at + LANES, head_size:] for u, at in block], axis=0)
        values = jnp.concatenate([values, jnp.ones_like(values)], axis=1)
        state = softmax_block(query, keys, values, state, scale)
    return state


def load(*arrays):
    keys, _, queries = arrays
    rows, head_size = keys.shape

    def kernel(key_ref, value_ref, query_ref, own_ref, queries_out, sems):
        copies = [
            pltpu.make_async_copy(key_ref, own_ref.at[:, pl.ds(0, head_size)], sems.at[0]),
            pltpu.make_async_copy(value_ref, own_ref.at[:, pl.ds(head_size, head_size)], sems.at[1]),
            pltpu.make_async_copy(query_ref, queries_out, sems.at[2]),
        ]
        for copy in copies:
            copy.start()
        for copy in copies:
            copy.wait()

    whole = pl.BlockSpec(memory_space=pltpu.HBM)
    vmem = pl.BlockSpec(memory_space=pltpu.VMEM)
    return pl.pallas_call(
        kernel,
        out_shape=(pltpu.VMEM((rows, 2 * head_size), keys.dtype), pltpu.VMEM(queries.shape, queries.dtype)),
        in_specs=[whole] * 3,
        out_specs=(vmem, vmem),
        scratch_shapes=[pltpu.SemaphoreType.DMA((3,))],
        compiler_params=pltpu.CompilerParams(vmem_limit_bytes=4 << 20),
    )(*[in_hbm(x) for x in arrays])


def attend(queries, units, state, out_weight, share):
    rows, width = queries.shape
    head_size = units[0].shape[1] // 2
    heads = width // head_size
    scale = head_size ** (-0.5) * math.log2(math.e)

    def kernel(*refs):
        query_ref, refs = refs[0], refs[1:]
        unit_refs, refs = refs[: len(units)], refs[len(units) :]
        weight_ref, top_out, sums_out, weight_out, sems = refs[-5:]
        fetch = Fetch(weight_ref, share[0], weight_out, sems)
        fetch.start()
        for h in range(heads):
            at = slice(h * rows, (h + 1) * rows)
            before = None if state is None else (refs[0][at], refs[1][at])
            top, sums = attend_head(h, query_ref, unit_refs, before, scale)
            top_out[at] = top
            sums_out[at] = sums
        fetch.wait()

    vmem = pl.BlockSpec(memory_space=pltpu.VMEM)
    args = [queries, *units, *(state or ())]
    *state, weight = pl.pallas_call(
        kernel,
        out_shape=(
            pltpu.VMEM((heads * rows, LANES), jnp.float32),
            pltpu.VMEM((heads * rows, 2 * head_size), jnp.float32),
            pltpu.VMEM((share[1], out_weight.shape[1]), out_weight.dtype),
        ),
        in_specs=[vmem] * len(args) + [pl.BlockSpec(memory_space=pltpu.HBM)],
        out_specs=(vmem, vmem, vmem),
        scratch_shapes=[pltpu.SemaphoreType.DMA((2,))],
        compiler_params=pltpu.CompilerParams(vmem_limit_bytes=16 << 20),
    )(*[in_vmem(x) for x in args], in_hbm(out_weight))
    return state, weight


def finish(queries, units, state, weights, out_weight):
    rows, width = queries.shape
    head_size = units[0].shape[1] // 2
    heads = width // head_size
    scale = head_size ** (-0.5) * math.log2(math.e)
    columns = out_weight.shape[1]
    begin = sum(w.shape[0] for w in weights)
    strip = math.gcd(columns, 512)
    strips = columns // strip

    def kernel(*refs):
        query_ref, refs = refs[0], refs[1:]
        unit_refs, refs = refs[: len(units)], refs[len(units) :]
        if state is not None:
            top_ref, sums_ref = refs[:2]
            refs = refs[2:]
        early, refs = refs[: len(weights)], refs[len(weights) :]
        weight_ref, out_ref, attended, staged, late, sems, late_sems = refs
        fetch = Fetch(weight_ref, begin, late, late_sems)
        fetch.start()
        for h in range(heads):
            at = slice(h * rows, (h + 1) * rows)
            before = None if state is None else (top_ref[at], sums_ref[at])
            _, sums = attend_head(h, query_ref, unit_refs, before, scale)
            attended[:, h * head_size : (h + 1) * head_size] = (
                sums[:, :head_size] / sums[:, head_size:]
            ).astype(jnp.bfloat16)
        left = attended[...]
        copies = []
        fetch.wait()
        for j in range(strips):
            at = slice(j * strip, (j + 1) * strip)
            right = jnp.concatenate([part[:, at] for part in (*early, late)], axis=0)
            staged[:, at] = jnp.dot(left, right, preferred_element_type=jnp.float32).astype(jnp.bfloat16)
            window = pl.ds(j * strip, strip)
            copy = pltpu.make_async_copy(staged.at[:, window], out_ref.at[:, window], sems.at[j])
            copy.start()
            copies.append(copy)
        for copy in copies:
            copy.wait()

    vmem = pl.BlockSpec(memory_space=pltpu.VMEM)
    whole = pl.BlockSpec(memory_space=pltpu.HBM)
    args = [queries, *units, *(state or ()), *weights]
    return pl.pallas_call(
        kernel,
        out_shape=jax.ShapeDtypeStruct((rows, columns), jnp.bfloat16),
        in_specs=[vmem] * len(args) + [whole],
        out_specs=whole,
        scratch_shapes=[
            pltpu.VMEM((rows, width), jnp.bfloat16),
            pltpu.VMEM((rows, columns), jnp.bfloat16),
            pltpu.VMEM((width - begin, columns), jnp.bfloat16),
            pltpu.SemaphoreType.DMA((strips,)),
            pltpu.SemaphoreType.DMA((2,)),
        ],
        compiler_params=pltpu.CompilerParams(vmem_limit_bytes=24 << 20),
    )(*[in_vmem(x) for x in args], in_hbm(out_weight))


def run_plan(own, queries, out_weight, size):
    low = 16
    if size > low:
        along = [[high * low + i for high in range(size // low)] for i in range(low)]
        own = lax.all_gather(own, "col", axis=0, tiled=True, axis_index_groups=along)
    rows = own.shape[0]
    known = {0: (0, own)}
    fresh = {0: own}
    heads = out_weight.shape[0] // (own.shape[1] // 2)
    state, weights, joined = None, [], None
    for kind, *what in PLAN:
        if kind == "hop":
            mask, held = what
            parts = []
            for m in held:
                at, array = known[m]
                parts.append(array if array.shape[0] == rows else array[at * rows : (at + 1) * rows])
            if len(parts) == 1:
                source = parts[0]
            else:
                if joined is not None:
                    parts, joined = lax.optimization_barrier((parts, joined))
                joined = source = jnp.concatenate(parts, axis=0)
            got = lax.ppermute(source, "col", [(j, j ^ mask) for j in range(size)])
            for at, m in enumerate(held):
                known[m ^ mask] = (at, got)
            fresh[held[0] ^ mask] = got
        else:
            units = [fresh.pop(m) for m in what[0] if m in fresh]
            count = what[1] * heads // 8 * (own.shape[1] // 2)
            begin = sum(w.shape[0] for w in weights)
            state, weight = attend(queries, units, state, out_weight, (begin, count))
            weights.append(weight)
    return finish(queries, list(fresh.values()), state, weights, out_weight)


def solution(mesh):
    size = mesh.shape["col"]

    def per_device(queries, keys, values, out_weight):
        own, queries = load(keys, values, queries)
        if size % 16:
            own = lax.all_gather(own, "col", axis=0, tiled=True)
            return finish(queries, [own], None, [], out_weight)
        return run_plan(own, queries, out_weight, size)

    spec = P(("groups", "col"), None)
    return jax.shard_map(
        per_device, mesh=mesh, in_specs=(spec, spec, spec, P()), out_specs=spec, check_vma=False
    )
```

time: 28.8 us -> 27.4 us (0.951)
  local copies, waits for them, and re-layouts: 5.29 us -> 0.04 us
  Pallas kernels: 4.92 us -> 7.58 us
  waiting for transfers between devices: 6.53 us -> 8.59 us
  starting transfers between devices: 11.7 us -> 10.8 us
    unnamed x5 -> x3, local copies, waits for them, and re-layouts: 4.52 us -> 0.02 us
    ppermute x11, waiting for transfers between devices: 6.53 us -> 8.59 us  [run_plan(): got = lax.ppermute(source, 'col', [(j, j ^ mask) for j in range(size)])]
    pallas_call x0 -> x1, Pallas kernels: none -> 1 us  [load(): pl.pallas_call(kernel, out_shape=(pltpu.VMEM((rows, 2 * head_size), keys....]
    pallas_call x2, Pallas kernels: 2.03 us -> 2.95 us  [attend(): pl.pallas_call(kernel, out_shape=(pltpu.VMEM((heads * rows, LANES), jnp.f...]
    ppermute x11, starting transfers between devices: 11.7 us -> 10.8 us  [run_plan(): got = lax.ppermute(source, 'col', [(j, j ^ mask) for j in range(size)])]
    concatenate x1 -> x3, local copies, waits for them, and re-layouts: 0.77 us -> 0.02 us  [run_plan(): joined = source = jnp.concatenate(parts, axis=0)]
    pallas_call x1, Pallas kernels: 2.88 us -> 3.63 us  [finish(): pl.pallas_call(kernel, out_shape=jax.ShapeDtypeStruct((rows, columns), jn...]
  transfers between devices with their start and end apart: 11 -> 11, of which waited for: 4 -> 3; matrix products, arithmetic and copies ran while one was open for 0% -> 0% of each run, Pallas kernels for 7% -> 11%
where the time goes in v2:
time: 27.4 us; the launch traced here: 27.1 us
  starting transfers between devices  10.8 us (39%)
  waiting for transfers between devices  8.59 us (31%)
  Pallas kernels  7.58 us (28%)
    ppermute x11, starting transfers between devices, run_plan(): got = lax.ppermute(source, 'col', [(j, j ^ mask) for j in range(size)])  10.8 us
    ppermute x11, waiting for transfers between devices, run_plan(): got = lax.ppermute(source, 'col', [(j, j ^ mask) for j in range(size)])  8.59 us
    pallas_call x1, Pallas kernels, finish(): pl.pallas_call(kernel, out_shape=jax.ShapeDtypeStruct((rows, columns), jn...  3.63 us
    pallas_call x2, Pallas kernels, attend(): pl.pallas_call(kernel, out_shape=(pltpu.VMEM((heads * rows, LANES), jnp.f...  2.95 us
    pallas_call x1, Pallas kernels, load(): pl.pallas_call(kernel, out_shape=(pltpu.VMEM((rows, 2 * head_size), keys....  1 us
  transfers between devices with their start and end apart: 11, of which 3 were waited for; matrix products, arithmetic and copies ran while one was open for 0% of the time, Pallas kernels for 11%

profile of v2, /device:TPU:0, one launch (start us, length us, event | category | flops | bytes accessed | tf_op | source)
XLA Modules:
  0.0 27.1 jit_solution(16997130519243456329)
XLA Ops:
  0.0 1.0 %shard_map.46 = (bf16[128,256]{1,0:T(8,128)(2,1)S(1)}, bf16[128,896]{1,0:T(8,128)(2,1)S(1)}) custom-call(bf16[128,128]{1,0:T(8,128)(2,1)} %key_ref.1, bf16[128,128]{1,0:T(8,128)(2,1)} %value_ref.1, bf16[128,896]{1,0:T(8,128)(2,1)} %query_ref.1), custom_call_target="tpu_custom_call" | custom-call | tf_op jit(solution)/shard_map/pallas_call | solution.py:112
  1.0 3.1 %collective-permute-start = (bf16[128,256]{1,0:T(8,128)(2,1)S(1)}, bf16[128,256]{1,0:T(8,128)(2,1)S(1)}, u32[]{:S(2)}, u32[]{:S(2)}) collective-permute-start(bf16[128,256]{1,0:T(8,128)(2,1)S(1)} %get-tuple-element.20.refs_1_), channel_id=1, source_target_pairs={{0,4},{1,5},{2,6},{3,7},{4,0},{5,1},{6,2},{7,3},{8,12},{9,13},{10,... | collective-permute-start | bytes 196616 | tf_op jit(solution)/shard_map/ppermute | solution.py:242
  4.1 2.6 %collective-permute-start.1 = (bf16[128,256]{1,0:T(8,128)(2,1)S(1)}, bf16[128,256]{1,0:T(8,128)(2,1)S(1)}, u32[]{:S(2)}, u32[]{:S(2)}) collective-permute-start(bf16[128,256]{1,0:T(8,128)(2,1)S(1)} %get-tuple-element.20.refs_1_), channel_id=1, source_target_pairs={{0,8},{1,9},{2,10},{3,11},{4,12},{5,13},{6,14},{7,15},{8,0},{9,1},... | collective-permute-start | bytes 196616 | tf_op jit(solution)/shard_map/ppermute | solution.py:242
  6.7 1.5 %collective-permute-start.5 = (bf16[128,256]{1,0:T(8,128)(2,1)S(1)}, bf16[128,256]{1,0:T(8,128)(2,1)S(1)}, u32[]{:S(2)}, u32[]{:S(2)}) collective-permute-start(bf16[128,256]{1,0:T(8,128)(2,1)S(1)} %get-tuple-element.20.refs_1_), channel_id=1, source_target_pairs={{0,2},{1,3},{2,0},{3,1},{4,6},{5,7},{6,4},{7,5},{8,10},{9,11},{10,... | collective-permute-start | bytes 196616 | tf_op jit(solution)/shard_map/ppermute | solution.py:242
  8.2 0.0 collective-permute-done.refs_3_
  8.2 1.8 %collective-permute-done.1.refs_4_ = bf16[128,256]{1,0:T(8,128)(2,1)S(1)} collective-permute-done((bf16[128,256]{1,0:T(8,128)(2,1)S(1)}, bf16[128,256]{1,0:T(8,128)(2,1)S(1)}, u32[]{:S(2)}, u32[]{:S(2)}) %collective-permute-start.1) | collective-permute-done | bytes 65568 | tf_op jit(solution)/shard_map/ppermute | solution.py:242
  10.0 1.5 %collective-permute-start.2 = (bf16[256,256]{1,0:T(8,128)(2,1)S(1)}, bf16[256,256]{1,0:T(8,128)(2,1)S(1)}, u32[]{:S(2)}, u32[]{:S(2)}) collective-permute-start(bf16[256,256]{1,0:T(8,128)(2,1)S(1)} %constant_dynamic-update-slice_fusion), channel_id=1, source_target_pairs={{0,2},{1,3},{2,0},{3,1},{4,6},{5,7},{6,4},{7,5},{8,10},{9,11},{10,... | collective-permute-start | bytes 393224 | tf_op jit(solution)/shard_map/ppermute | solution.py:242
  11.6 0.0 collective-permute-done.5.refs_1_
  11.6 0.4 %collective-permute-start.3 = (bf16[128,256]{1,0:T(8,128)(2,1)S(1)}, bf16[128,256]{1,0:T(8,128)(2,1)S(1)}, u32[]{:S(2)}, u32[]{:S(2)}) collective-permute-start(bf16[128,256]{1,0:T(8,128)(2,1)S(1)} %collective-permute-done.1.refs_4_), channel_id=1, source_target_pairs={{0,4},{1,5},{2,6},{3,7},{4,0},{5,1},{6,2},{7,3},{8,12},{9,13},{10,... | collective-permute-start | bytes 196616 | tf_op jit(solution)/shard_map/ppermute | solution.py:242
  12.0 0.0 collective-permute-start.8
  12.0 3.9 %collective-permute-done.3.refs_6_ = bf16[128,256]{1,0:T(8,128)(2,1)S(1)} collective-permute-done((bf16[128,256]{1,0:T(8,128)(2,1)S(1)}, bf16[128,256]{1,0:T(8,128)(2,1)S(1)}, u32[]{:S(2)}, u32[]{:S(2)}) %collective-permute-start.3) | collective-permute-done | bytes 65568 | tf_op jit(solution)/shard_map/ppermute | solution.py:242
  15.9 0.1 collective-permute-start.9
  16.0 1.0 %collective-permute-start.4 = (bf16[128,256]{1,0:T(8,128)(2,1)S(1)}, bf16[128,256]{1,0:T(8,128)(2,1)S(1)}, u32[]{:S(2)}, u32[]{:S(2)}) collective-permute-start(bf16[128,256]{1,0:T(8,128)(2,1)S(1)} %collective-permute-done.3.refs_6_), channel_id=1, source_target_pairs={{0,2},{1,3},{2,0},{3,1},{4,6},{5,7},{6,4},{7,5},{8,10},{9,11},{10,... | collective-permute-start | bytes 196616 | tf_op jit(solution)/shard_map/ppermute | solution.py:242
  17.0 0.0 collective-permute-done.2.refs_1_
  17.1 0.2 collective-permute-start.6
  17.3 0.4 %collective-permute-start.10 = (bf16[128,256]{1,0:T(8,128)(2,1)S(1)}, bf16[128,256]{1,0:T(8,128)(2,1)S(1)}, u32[]{:S(2)}, u32[]{:S(2)}) collective-permute-start(bf16[128,256]{1,0:T(8,128)(2,1)S(1)} %get-tuple-element.20.refs_1_), channel_id=1, source_target_pairs={{0,1},{1,0},{2,3},{3,2},{4,5},{5,4},{6,7},{7,6},{8,9},{9,8},{10,11... | collective-permute-start | bytes 196616 | tf_op jit(solution)/shard_map/ppermute | solution.py:242
  17.6 2.9 %collective-permute-done.4.refs_2_ = bf16[128,256]{1,0:T(8,128)(2,1)S(1)} collective-permute-done((bf16[128,256]{1,0:T(8,128)(2,1)S(1)}, bf16[128,256]{1,0:T(8,128)(2,1)S(1)}, u32[]{:S(2)}, u32[]{:S(2)}) %collective-permute-start.4) | collective-permute-done | bytes 65568 | tf_op jit(solution)/shard_map/ppermute | solution.py:242
  20.5 0.0 collective-permute-start.7
  20.5 0.0 collective-permute-done.10.refs_2_
  20.5 1.2 %shard_map.47 = (f32[896,128]{1,0:T(8,128)S(1)}, f32[896,256]{1,0:T(8,128)S(1)}, bf16[128,3584]{1,0:T(8,128)(2,1)S(1)}) custom-call(bf16[128,896]{1,0:T(8,128)(2,1)S(1)} %get-tuple-element.19.refs_0_, bf16[128,256]{1,0:T(8,128)(2,1)S(1)} %get-tuple-element.20.refs_1_, bf16[128,256]{1,0:T(8,128)(2,1)S(1)} %collective-permute-done.10.refs_2_, ...), custom_call_target="tpu_custom_call" | custom-call | tf_op jit(solution)/shard_map/pallas_call | solution.py:144
  21.7 0.0 collective-permute-done.8.refs_2_
  21.7 0.0 collective-permute-done.9.refs_5_
  21.7 1.8 %shard_map.48 = (f32[896,128]{1,0:T(8,128)S(1)}, f32[896,256]{1,0:T(8,128)S(1)}, bf16[384,3584]{1,0:T(8,128)(2,1)S(1)}) custom-call(bf16[128,896]{1,0:T(8,128)(2,1)S(1)} %get-tuple-element.19.refs_0_, bf16[128,256]{1,0:T(8,128)(2,1)S(1)} %collective-permute-done.5.refs_1_, bf16[256,256]{1,0:T(8,128)(2,1)S(1)} %collective-permute-done.8.refs_2_, ...), custom_call_target="tpu_custom_call" | custom-call | tf_op jit(solution)/shard_map/pallas_call | solution.py:144
  23.5 0.0 collective-permute-done.7.refs_4_
  23.5 0.0 collective-permute-done.6.refs_3_
  23.5 3.6 %shard_map.49 = bf16[128,3584]{1,0:T(8,128)(2,1)} custom-call(bf16[128,896]{1,0:T(8,128)(2,1)S(1)} %get-tuple-element.19.refs_0_, bf16[256,256]{1,0:T(8,128)(2,1)S(1)} %collective-permute-done.2.refs_1_, bf16[128,256]{1,0:T(8,128)(2,1)S(1)} %collective-permute-done.4.refs_2_, bf16[256,256]{1,0:T(8,128)(2,1)S(1)} %collective-permute-done.6.refs_3_, ...), custom_call_target="tpu_custom_call" | custom-call | tf_op jit(solution)/shard_map/pallas_call | solution.py:203
  (8 shorter events, 0.1 us)
Async XLA Ops:
  1.0 7.2 %collective-permute-start = (bf16[128,256]{1,0:T(8,128)(2,1)S(1)}, bf16[128,256]{1,0:T(8,128)(2,1)S(1)}, u32[]{:S(2)}, u32[]{:S(2)}) collective-permute-start(bf16[128,256]{1,0:T(8,128)(2,1)S(1)} %get-tuple-element.20.refs_1_), channel_id=1, source_target_pairs={{0,4},{1,5},{2,6},{3,7},{4,0},{5,1},{6,2},{7,3},{8,12},{9,13},{10,... | collective-permute-start | bytes 196616 | tf_op jit(solution)/shard_map/ppermute | solution.py:242
  4.1 5.9 %collective-permute-start.1 = (bf16[128,256]{1,0:T(8,128)(2,1)S(1)}, bf16[128,256]{1,0:T(8,128)(2,1)S(1)}, u32[]{:S(2)}, u32[]{:S(2)}) collective-permute-start(bf16[128,256]{1,0:T(8,128)(2,1)S(1)} %get-tuple-element.20.refs_1_), channel_id=1, source_target_pairs={{0,8},{1,9},{2,10},{3,11},{4,12},{5,13},{6,14},{7,15},{8,0},{9,1},... | collective-permute-start | bytes 196616 | tf_op jit(solution)/shard_map/ppermute | solution.py:242
  6.7 4.8 %collective-permute-start.5 = (bf16[128,256]{1,0:T(8,128)(2,1)S(1)}, bf16[128,256]{1,0:T(8,128)(2,1)S(1)}, u32[]{:S(2)}, u32[]{:S(2)}) collective-permute-start(bf16[128,256]{1,0:T(8,128)(2,1)S(1)} %get-tuple-element.20.refs_1_), channel_id=1, source_target_pairs={{0,2},{1,3},{2,0},{3,1},{4,6},{5,7},{6,4},{7,5},{8,10},{9,11},{10,... | collective-permute-start | bytes 196616 | tf_op jit(solution)/shard_map/ppermute | solution.py:242
  10.0 7.0 %collective-permute-start.2 = (bf16[256,256]{1,0:T(8,128)(2,1)S(1)}, bf16[256,256]{1,0:T(8,128)(2,1)S(1)}, u32[]{:S(2)}, u32[]{:S(2)}) collective-permute-start(bf16[256,256]{1,0:T(8,128)(2,1)S(1)} %constant_dynamic-update-slice_fusion), channel_id=1, source_target_pairs={{0,2},{1,3},{2,0},{3,1},{4,6},{5,7},{6,4},{7,5},{8,10},{9,11},{10,... | collective-permute-start | bytes 393224 | tf_op jit(solution)/shard_map/ppermute | solution.py:242
  11.6 4.3 %collective-permute-start.3 = (bf16[128,256]{1,0:T(8,128)(2,1)S(1)}, bf16[128,256]{1,0:T(8,128)(2,1)S(1)}, u32[]{:S(2)}, u32[]{:S(2)}) collective-permute-start(bf16[128,256]{1,0:T(8,128)(2,1)S(1)} %collective-permute-done.1.refs_4_), channel_id=1, source_target_pairs={{0,4},{1,5},{2,6},{3,7},{4,0},{5,1},{6,2},{7,3},{8,12},{9,13},{10,... | collective-permute-start | bytes 196616 | tf_op jit(solution)/shard_map/ppermute | solution.py:242
  12.0 9.7 %collective-permute-start.8 = (bf16[256,256]{1,0:T(8,128)(2,1)S(1)}, bf16[256,256]{1,0:T(8,128)(2,1)S(1)}, u32[]{:S(2)}, u32[]{:S(2)}) collective-permute-start(bf16[256,256]{1,0:T(8,128)(2,1)S(1)} %constant_dynamic-update-slice_fusion.2), channel_id=1, source_target_pairs={{0,1},{1,0},{2,3},{3,2},{4,5},{5,4},{6,7},{7,6},{8,9},{9,8},{10,11... | collective-permute-start | bytes 393224 | tf_op jit(solution)/shard_map/ppermute | solution.py:242
  15.9 5.8 %collective-permute-start.9 = (bf16[256,256]{1,0:T(8,128)(2,1)S(1)}, bf16[256,256]{1,0:T(8,128)(2,1)S(1)}, u32[]{:S(2)}, u32[]{:S(2)}) collective-permute-start(bf16[256,256]{1,0:T(8,128)(2,1)S(1)} %constant_dynamic-update-slice_fusion.4), channel_id=1, source_target_pairs={{0,1},{1,0},{2,3},{3,2},{4,5},{5,4},{6,7},{7,6},{8,9},{9,8},{10,11... | collective-permute-start | bytes 393224 | tf_op jit(solution)/shard_map/ppermute | solution.py:242
  16.0 4.5 %collective-permute-start.4 = (bf16[128,256]{1,0:T(8,128)(2,1)S(1)}, bf16[128,256]{1,0:T(8,128)(2,1)S(1)}, u32[]{:S(2)}, u32[]{:S(2)}) collective-permute-start(bf16[128,256]{1,0:T(8,128)(2,1)S(1)} %collective-permute-done.3.refs_6_), channel_id=1, source_target_pairs={{0,2},{1,3},{2,0},{3,1},{4,6},{5,7},{6,4},{7,5},{8,10},{9,11},{10,... | collective-permute-start | bytes 196616 | tf_op jit(solution)/shard_map/ppermute | solution.py:242
  17.1 6.5 %collective-permute-start.6 = (bf16[256,256]{1,0:T(8,128)(2,1)S(1)}, bf16[256,256]{1,0:T(8,128)(2,1)S(1)}, u32[]{:S(2)}, u32[]{:S(2)}) collective-permute-start(bf16[256,256]{1,0:T(8,128)(2,1)S(1)} %pad_maximum_fusion), channel_id=1, source_target_pairs={{0,1},{1,0},{2,3},{3,2},{4,5},{5,4},{6,7},{7,6},{8,9},{9,8},{10,11... | collective-permute-start | bytes 393224 | tf_op jit(solution)/shard_map/ppermute | solution.py:242
  17.3 3.2 %collective-permute-start.10 = (bf16[128,256]{1,0:T(8,128)(2,1)S(1)}, bf16[128,256]{1,0:T(8,128)(2,1)S(1)}, u32[]{:S(2)}, u32[]{:S(2)}) collective-permute-start(bf16[128,256]{1,0:T(8,128)(2,1)S(1)} %get-tuple-element.20.refs_1_), channel_id=1, source_target_pairs={{0,1},{1,0},{2,3},{3,2},{4,5},{5,4},{6,7},{7,6},{8,9},{9,8},{10,11... | collective-permute-start | bytes 196616 | tf_op jit(solution)/shard_map/ppermute | solution.py:242
  20.5 3.0 %collective-permute-start.7 = (bf16[128,256]{1,0:T(8,128)(2,1)S(1)}, bf16[128,256]{1,0:T(8,128)(2,1)S(1)}, u32[]{:S(2)}, u32[]{:S(2)}) collective-permute-start(bf16[128,256]{1,0:T(8,128)(2,1)S(1)} %collective-permute-done.4.refs_2_), channel_id=1, source_target_pairs={{0,1},{1,0},{2,3},{3,2},{4,5},{5,4},{6,7},{7,6},{8,9},{9,8},{10,11... | collective-permute-start | bytes 196616 | tf_op jit(solution)/shard_map/ppermute | solution.py:242

commit v3 on v2

v3 whole, which is shorter than its diff:
```python
import math

import jax
import jax.numpy as jnp
from jax import lax
from jax.experimental import pallas as pl
from jax.experimental.pallas import tpu as pltpu
from jax.sharding import PartitionSpec as P

LANES = 128
BLOCK = 1024
PLAN = (
    ("hop", 8, (0,)),
    ("hop", 12, (0,)),
    ("hop", 2, (0,)),
    ("hop", 1, (0,)),
    ("hop", 4, (0,)),
    ("hop", 4, (2,)),
    ("hop", 2, (8, 12)),
    ("attend", (0, 1)),
    ("hop", 1, (2, 4, 8, 12)),
    ("attend", (2, 4, 8, 12)),
    ("hop", 1, (6, 10, 14)),
    ("attend", (3, 5, 9, 13, 6, 10, 14)),
)


def in_vmem(x):
    return pltpu.with_memory_space_constraint(x, pltpu.VMEM)


def in_hbm(x):
    return pltpu.with_memory_space_constraint(x, pltpu.HBM)


def softmax_block(query, keys, values, state, scale):
    rows = query.shape[0]
    tiles = keys.shape[0] // LANES
    scores = lax.dot_general(query, keys, (((1,), (1,)), ((), ())), preferred_element_type=jnp.float32)
    parts = [scores[:, i * LANES : (i + 1) * LANES] for i in range(tiles)]
    peak = parts[0]
    for part in parts[1:]:
        peak = jnp.maximum(peak, part)
    top = jnp.broadcast_to(jnp.max(peak, axis=1, keepdims=True), (rows, LANES))
    if state is not None:
        top = jnp.maximum(top, state[0])
    weights = jnp.concatenate(
        [jnp.exp2((part - top) * scale).astype(jnp.bfloat16) for part in parts], axis=1
    )
    sums = jnp.dot(weights, values, preferred_element_type=jnp.float32)
    if state is not None:
        fade = jnp.exp2((state[0] - top) * scale)
        sums = sums + state[1] * jnp.concatenate([fade, fade], axis=1)
    return top, sums


def attend_head(h, query_ref, unit_refs, state, scale):
    head_size = unit_refs[0].shape[1] // 2
    query = query_ref[:, h * head_size : (h + 1) * head_size]
    pieces = [(u, at) for u in unit_refs for at in range(0, u.shape[0], LANES)]
    step = BLOCK // LANES
    for start in range(0, len(pieces), step):
        block = pieces[start : start + step]
        keys = jnp.concatenate([u[at : at + LANES, :head_size] for u, at in block], axis=0)
        values = jnp.concatenate([u[at : at + LANES, head_size:] for u, at in block], axis=0)
        values = jnp.concatenate([values, jnp.ones_like(values)], axis=1)
        state = softmax_block(query, keys, values, state, scale)
    return state


def load(*arrays):
    keys, _, queries = arrays
    rows, head_size = keys.shape

    def kernel(key_ref, value_ref, query_ref, own_ref, queries_out, sems):
        copies = [
            pltpu.make_async_copy(key_ref, own_ref.at[:, pl.ds(0, head_size)], sems.at[0]),
            pltpu.make_async_copy(value_ref, own_ref.at[:, pl.ds(head_size, head_size)], sems.at[1]),
            pltpu.make_async_copy(query_ref, queries_out, sems.at[2]),
        ]
        for copy in copies:
            copy.start()
        for copy in copies:
            copy.wait()

    whole = pl.BlockSpec(memory_space=pltpu.HBM)
    vmem = pl.BlockSpec(memory_space=pltpu.VMEM)
    return pl.pallas_call(
        kernel,
        out_shape=(pltpu.VMEM((rows, 2 * head_size), keys.dtype), pltpu.VMEM(queries.shape, queries.dtype)),
        in_specs=[whole] * 3,
        out_specs=(vmem, vmem),
        scratch_shapes=[pltpu.SemaphoreType.DMA((3,))],
        compiler_params=pltpu.CompilerParams(vmem_limit_bytes=4 << 20),
    )(*[in_hbm(x) for x in arrays])


def attend(queries, units, state, last=False):
    rows, width = queries.shape
    head_size = units[0].shape[1] // 2
    heads = width // head_size
    scale = head_size ** (-0.5) * math.log2(math.e)

    def kernel(*refs):
        query_ref, refs = refs[0], refs[1:]
        unit_refs, refs = refs[: len(units)], refs[len(units) :]
        for h in range(heads):
            at = slice(h * rows, (h + 1) * rows)
            before = None if state is None else (refs[0][at], refs[1][at])
            top, sums = attend_head(h, query_ref, unit_refs, before, scale)
            if last:
                refs[-1][:, h * head_size : (h + 1) * head_size] = (
                    sums[:, :head_size] / sums[:, head_size:]
                ).astype(jnp.bfloat16)
            else:
                refs[-2][at] = top
                refs[-1][at] = sums

    vmem = pl.BlockSpec(memory_space=pltpu.VMEM)
    args = [queries, *units, *(state or ())]
    if last:
        out_shape = pltpu.VMEM((rows, width), jnp.bfloat16)
    else:
        out_shape = (
            pltpu.VMEM((heads * rows, LANES), jnp.float32),
            pltpu.VMEM((heads * rows, 2 * head_size), jnp.float32),
        )
    return pl.pallas_call(
        kernel,
        out_shape=out_shape,
        in_specs=[vmem] * len(args),
        out_specs=vmem if last else (vmem, vmem),
        compiler_params=pltpu.CompilerParams(vmem_limit_bytes=16 << 20),
    )(*[in_vmem(x) for x in args])


def project(attended, out_weight):
    return jnp.dot(attended, out_weight, preferred_element_type=jnp.float32).astype(jnp.bfloat16)


def run_plan(own, queries, size):
    low = 16
    if size > low:
        along = [[high * low + i for high in range(size // low)] for i in range(low)]
        own = lax.all_gather(own, "col", axis=0, tiled=True, axis_index_groups=along)
    rows = own.shape[0]
    known = {0: (0, own)}
    fresh = {0: own}
    state, joined = None, None
    for kind, *what in PLAN:
        if kind == "hop":
            mask, held = what
            parts = []
            for m in held:
                at, array = known[m]
                parts.append(array if array.shape[0] == rows else array[at * rows : (at + 1) * rows])
            if len(parts) == 1:
                source = parts[0]
            else:
                if joined is not None:
                    parts, joined = lax.optimization_barrier((parts, joined))
                joined = source = jnp.concatenate(parts, axis=0)
            got = lax.ppermute(source, "col", [(j, j ^ mask) for j in range(size)])
            for at, m in enumerate(held):
                known[m ^ mask] = (at, got)
            fresh[held[0] ^ mask] = got
        else:
            units = [fresh.pop(m) for m in what[0] if m in fresh]
            state = attend(queries, units, state)
    return attend(queries, list(fresh.values()), state, True)


def solution(mesh):
    size = mesh.shape["col"]

    def per_device(queries, keys, values, out_weight):
        own, queries = load(keys, values, queries)
        if size % 16:
            own = lax.all_gather(own, "col", axis=0, tiled=True)
            return project(attend(queries, [own], None, True), out_weight)
        return project(run_plan(own, queries, size), out_weight)

    spec = P(("groups", "col"), None)
    return jax.shard_map(
        per_device, mesh=mesh, in_specs=(spec, spec, spec, P()), out_specs=spec, check_vma=False
    )
```

time: 27.4 us -> 25.9 us (0.945)
  Pallas kernels: 7.58 us -> 5.04 us
  matrix products: 0 us -> 2.05 us
  starting transfers between devices: 10.8 us -> 8.8 us
  waiting for transfers between devices: 8.59 us -> 9.68 us
    pallas_call x3 -> x4, Pallas kernels: 6.58 us -> 3.89 us  [attend(): pl.pallas_call(kernel, out_shape=out_shape, in_specs=[vmem] * len(args),...]
    dot_general x0 -> x1, matrix products: none -> 2.05 us  [project(): jnp.dot(attended, out_weight, preferred_element_type=jnp.float32)]
    ppermute x11 -> x9, starting transfers between devices: 10.8 us -> 8.8 us  [run_plan(): got = lax.ppermute(source, 'col', [(j, j ^ mask) for j in range(size)])]
    ppermute x11 -> x9, waiting for transfers between devices: 8.59 us -> 9.68 us  [run_plan(): got = lax.ppermute(source, 'col', [(j, j ^ mask) for j in range(size)])]
  transfers between devices with their start and end apart: 11 -> 9, of which waited for: 3 -> 5; matrix products, arithmetic and copies ran while one was open for 0% -> 0% of each run, Pallas kernels for 11% -> 12%
where the time goes in v3:
time: 25.9 us; the launch traced here: 25.7 us
  waiting for transfers between devices  9.68 us (37%)
  starting transfers between devices  8.8 us (34%)
  Pallas kernels  5.04 us (19%)
  matrix products  2.05 us (8%)
    ppermute x9, waiting for transfers between devices, run_plan(): got = lax.ppermute(source, 'col', [(j, j ^ mask) for j in range(size)])  9.68 us
    ppermute x9, starting transfers between devices, run_plan(): got = lax.ppermute(source, 'col', [(j, j ^ mask) for j in range(size)])  8.8 us
    pallas_call x4, Pallas kernels, attend(): pl.pallas_call(kernel, out_shape=out_shape, in_specs=[vmem] * len(args),...  3.89 us
    dot_general x1, matrix products, project(): jnp.dot(attended, out_weight, preferred_element_type=jnp.float32)  2.05 us
    pallas_call x1, Pallas kernels, load(): pl.pallas_call(kernel, out_shape=(pltpu.VMEM((rows, 2 * head_size), keys....  1.15 us
  transfers between devices with their start and end apart: 9, of which 5 were waited for; matrix products, arithmetic and copies ran while one was open for 0% of the time, Pallas kernels for 12%

profile of v3, /device:TPU:0, one launch (start us, length us, event | category | flops | bytes accessed | tf_op | source)
XLA Modules:
  0.0 25.7 jit_solution(7893358115196413780)
XLA Ops:
  0.0 0.0 copy-start
  0.0 1.1 %shard_map.46 = (bf16[128,256]{1,0:T(8,128)(2,1)S(1)}, bf16[128,896]{1,0:T(8,128)(2,1)S(1)}) custom-call(bf16[128,128]{1,0:T(8,128)(2,1)} %key_ref.1, bf16[128,128]{1,0:T(8,128)(2,1)} %value_ref.1, bf16[128,896]{1,0:T(8,128)(2,1)} %query_ref.1), custom_call_target="tpu_custom_call" | custom-call | tf_op jit(solution)/shard_map/pallas_call | solution.py:88
  1.2 4.1 %collective-permute-start.2 = (bf16[128,256]{1,0:T(8,128)(2,1)S(1)}, bf16[128,256]{1,0:T(8,128)(2,1)S(1)}, u32[]{:S(2)}, u32[]{:S(2)}) collective-permute-start(bf16[128,256]{1,0:T(8,128)(2,1)S(1)} %get-tuple-element.21.refs_1_), channel_id=1, source_target_pairs={{0,8},{1,9},{2,10},{3,11},{4,12},{5,13},{6,14},{7,15},{8,0},{9,1},... | collective-permute-start | bytes 196616 | tf_op jit(solution)/shard_map/ppermute | solution.py:163
  5.3 1.5 %collective-permute-start = (bf16[128,256]{1,0:T(8,128)(2,1)S(1)}, bf16[128,256]{1,0:T(8,128)(2,1)S(1)}, u32[]{:S(2)}, u32[]{:S(2)}) collective-permute-start(bf16[128,256]{1,0:T(8,128)(2,1)S(1)} %get-tuple-element.21.refs_1_), channel_id=1, source_target_pairs={{0,2},{1,3},{2,0},{3,1},{4,6},{5,7},{6,4},{7,5},{8,10},{9,11},{10,... | collective-permute-start | bytes 196616 | tf_op jit(solution)/shard_map/ppermute | solution.py:163
  6.8 1.3 %collective-permute-start.3 = (bf16[128,256]{1,0:T(8,128)(2,1)S(1)}, bf16[128,256]{1,0:T(8,128)(2,1)S(1)}, u32[]{:S(2)}, u32[]{:S(2)}) collective-permute-start(bf16[128,256]{1,0:T(8,128)(2,1)S(1)} %get-tuple-element.21.refs_1_), channel_id=1, source_target_pairs={{0,12},{1,13},{2,14},{3,15},{4,8},{5,9},{6,10},{7,11},{8,4},{9,5},... | collective-permute-start | bytes 196616 | tf_op jit(solution)/shard_map/ppermute | solution.py:163
  8.2 0.2 collective-permute-start.5
  8.4 0.5 %collective-permute-done.2.refs_3_ = bf16[128,256]{1,0:T(8,128)(2,1)S(1)} collective-permute-done((bf16[128,256]{1,0:T(8,128)(2,1)S(1)}, bf16[128,256]{1,0:T(8,128)(2,1)S(1)}, u32[]{:S(2)}, u32[]{:S(2)}) %collective-permute-start.2) | collective-permute-done | bytes 65568 | tf_op jit(solution)/shard_map/ppermute | solution.py:163
  8.9 4.0 %collective-permute-done.3.refs_4_ = bf16[128,256]{1,0:T(8,128)(2,1)S(1)} collective-permute-done((bf16[128,256]{1,0:T(8,128)(2,1)S(1)}, bf16[128,256]{1,0:T(8,128)(2,1)S(1)}, u32[]{:S(2)}, u32[]{:S(2)}) %collective-permute-start.3) | collective-permute-done | bytes 65568 | tf_op jit(solution)/shard_map/ppermute | solution.py:163
  13.0 0.5 %collective-permute-start.4 = (bf16[256,256]{1,0:T(8,128)(2,1)S(1)}, bf16[256,256]{1,0:T(8,128)(2,1)S(1)}, u32[]{:S(2)}, u32[]{:S(2)}) collective-permute-start(bf16[256,256]{1,0:T(8,128)(2,1)S(1)} %constant_dynamic-update-slice_fusion), channel_id=1, source_target_pairs={{0,2},{1,3},{2,0},{3,1},{4,6},{5,7},{6,4},{7,5},{8,10},{9,11},{10,... | collective-permute-start | bytes 393224 | tf_op jit(solution)/shard_map/ppermute | solution.py:163
  13.5 0.0 collective-permute-done.refs_1_
  13.5 0.0 collective-permute-done.5.refs_2_
  13.5 0.1 collective-permute-start.7
  13.6 0.4 %collective-permute-start.1 = (bf16[128,256]{1,0:T(8,128)(2,1)S(1)}, bf16[128,256]{1,0:T(8,128)(2,1)S(1)}, u32[]{:S(2)}, u32[]{:S(2)}) collective-permute-start(bf16[128,256]{1,0:T(8,128)(2,1)S(1)} %collective-permute-done.refs_1_), channel_id=1, source_target_pairs={{0,4},{1,5},{2,6},{3,7},{4,0},{5,1},{6,2},{7,3},{8,12},{9,13},{10,... | collective-permute-start | bytes 196616 | tf_op jit(solution)/shard_map/ppermute | solution.py:163
  14.0 3.9 %collective-permute-done.4.refs_3_ = bf16[256,256]{1,0:T(8,128)(2,1)S(1)} collective-permute-done((bf16[256,256]{1,0:T(8,128)(2,1)S(1)}, bf16[256,256]{1,0:T(8,128)(2,1)S(1)}, u32[]{:S(2)}, u32[]{:S(2)}) %collective-permute-start.4) | collective-permute-done | bytes 131104 | tf_op jit(solution)/shard_map/ppermute | solution.py:163
  18.0 0.2 collective-permute-done.1.refs_2_
  18.1 0.1 collective-permute-start.6
  18.2 0.5 %collective-permute-start.8 = (bf16[128,256]{1,0:T(8,128)(2,1)S(1)}, bf16[128,256]{1,0:T(8,128)(2,1)S(1)}, u32[]{:S(2)}, u32[]{:S(2)}) collective-permute-start(bf16[128,256]{1,0:T(8,128)(2,1)S(1)} %get-tuple-element.21.refs_1_), channel_id=1, source_target_pairs={{0,1},{1,0},{2,3},{3,2},{4,5},{5,4},{6,7},{7,6},{8,9},{9,8},{10,11... | collective-permute-start | bytes 196616 | tf_op jit(solution)/shard_map/ppermute | solution.py:163
  18.7 1.0 %collective-permute-done.8.refs_2_ = bf16[128,256]{1,0:T(8,128)(2,1)S(1)} collective-permute-done((bf16[128,256]{1,0:T(8,128)(2,1)S(1)}, bf16[128,256]{1,0:T(8,128)(2,1)S(1)}, u32[]{:S(2)}, u32[]{:S(2)}) %collective-permute-start.8) | collective-permute-done | bytes 65568 | tf_op jit(solution)/shard_map/ppermute | solution.py:163
  19.7 0.6 %shard_map.47 = (f32[896,128]{1,0:T(8,128)S(1)}, f32[896,256]{1,0:T(8,128)S(1)}) custom-call(bf16[128,896]{1,0:T(8,128)(2,1)S(1)} %get-tuple-element.20.refs_0_, bf16[128,256]{1,0:T(8,128)(2,1)S(1)} %get-tuple-element.21.refs_1_, bf16[128,256]{1,0:T(8,128)(2,1)S(1)} %collective-permute-done.8.refs_2_), custom_call_target="tpu_custom_call" | custom-call | tf_op jit(solution)/shard_map/pallas_call | solution.py:128
  20.3 0.9 %shard_map.48 = (f32[896,128]{1,0:T(8,128)S(1)}, f32[896,256]{1,0:T(8,128)S(1)}) custom-call(bf16[128,896]{1,0:T(8,128)(2,1)S(1)} %get-tuple-element.20.refs_0_, bf16[128,256]{1,0:T(8,128)(2,1)S(1)} %collective-permute-done.refs_1_, bf16[128,256]{1,0:T(8,128)(2,1)S(1)} %collective-permute-done.5.refs_2_, ...), custom_call_target="tpu_custom_call" | custom-call | tf_op jit(solution)/shard_map/pallas_call | solution.py:128
  21.2 0.0 collective-permute-done.7.refs_1_
  21.2 1.5 %shard_map.49 = (f32[896,128]{1,0:T(8,128)S(1)}, f32[896,256]{1,0:T(8,128)S(1)}) custom-call(bf16[128,896]{1,0:T(8,128)(2,1)S(1)} %get-tuple-element.20.refs_0_, bf16[512,256]{1,0:T(8,128)(2,1)S(1)} %collective-permute-done.7.refs_1_, bf16[128,256]{1,0:T(8,128)(2,1)S(1)} %collective-permute-done.1.refs_2_, ...), custom_call_target="tpu_custom_call" | custom-call | tf_op jit(solution)/shard_map/pallas_call | solution.py:128
  22.7 0.0 collective-permute-done.6.refs_1_
  22.7 0.9 %shard_map.50 = bf16[128,896]{1,0:T(8,128)(2,1)S(1)} custom-call(bf16[128,896]{1,0:T(8,128)(2,1)S(1)} %get-tuple-element.20.refs_0_, bf16[384,256]{1,0:T(8,128)(2,1)S(1)} %collective-permute-done.6.refs_1_, f32[896,128]{1,0:T(8,128)S(1)} %get-tuple-element.33.refs_2_, f32[896,256]{1,0:T(8,128)S(1)} %get-tuple-element.34.refs_3_), custom_call_target="tpu_custom_call" | custom-call | tf_op jit(solution)/shard_map/pallas_call | solution.py:128
  23.7 0.0 copy-done
  23.7 2.1 %convolution_convert_fusion = bf16[128,3584]{1,0:T(8,128)(2,1)} fusion(bf16[128,896]{1,0:T(8,128)(2,1)S(1)} %shard_map.50, bf16[896,3584]{1,0:T(8,128)(2,1)S(1)} %copy-done), kind=kOutput, calls=%fused_computation | convolution fusion | flops 822542336 | bytes 7569408 | tf_op jit(solution)/shard_map/dot_general | solution.py:138
  (8 shorter events, 0.1 us)
Async XLA Ops:
  0.0 23.7 %copy-start = (bf16[896,3584]{1,0:T(8,128)(2,1)S(1)}, bf16[896,3584]{1,0:T(8,128)(2,1)}, u32[]{:S(2)}) copy-start(bf16[896,3584]{1,0:T(8,128)(2,1)} %param.7) | copy-start | bytes 19267588
  1.2 7.8 %collective-permute-start.2 = (bf16[128,256]{1,0:T(8,128)(2,1)S(1)}, bf16[128,256]{1,0:T(8,128)(2,1)S(1)}, u32[]{:S(2)}, u32[]{:S(2)}) collective-permute-start(bf16[128,256]{1,0:T(8,128)(2,1)S(1)} %get-tuple-element.21.refs_1_), channel_id=1, source_target_pairs={{0,8},{1,9},{2,10},{3,11},{4,12},{5,13},{6,14},{7,15},{8,0},{9,1},... | collective-permute-start | bytes 196616 | tf_op jit(solution)/shard_map/ppermute | solution.py:163
  5.3 8.2 %collective-permute-start = (bf16[128,256]{1,0:T(8,128)(2,1)S(1)}, bf16[128,256]{1,0:T(8,128)(2,1)S(1)}, u32[]{:S(2)}, u32[]{:S(2)}) collective-permute-start(bf16[128,256]{1,0:T(8,128)(2,1)S(1)} %get-tuple-element.21.refs_1_), channel_id=1, source_target_pairs={{0,2},{1,3},{2,0},{3,1},{4,6},{5,7},{6,4},{7,5},{8,10},{9,11},{10,... | collective-permute-start | bytes 196616 | tf_op jit(solution)/shard_map/ppermute | solution.py:163
  6.8 6.2 %collective-permute-start.3 = (bf16[128,256]{1,0:T(8,128)(2,1)S(1)}, bf16[128,256]{1,0:T(8,128)(2,1)S(1)}, u32[]{:S(2)}, u32[]{:S(2)}) collective-permute-start(bf16[128,256]{1,0:T(8,128)(2,1)S(1)} %get-tuple-element.21.refs_1_), channel_id=1, source_target_pairs={{0,12},{1,13},{2,14},{3,15},{4,8},{5,9},{6,10},{7,11},{8,4},{9,5},... | collective-permute-start | bytes 196616 | tf_op jit(solution)/shard_map/ppermute | solution.py:163
  8.2 5.3 %collective-permute-start.5 = (bf16[128,256]{1,0:T(8,128)(2,1)S(1)}, bf16[128,256]{1,0:T(8,128)(2,1)S(1)}, u32[]{:S(2)}, u32[]{:S(2)}) collective-permute-start(bf16[128,256]{1,0:T(8,128)(2,1)S(1)} %get-tuple-element.21.refs_1_), channel_id=1, source_target_pairs={{0,4},{1,5},{2,6},{3,7},{4,0},{5,1},{6,2},{7,3},{8,12},{9,13},{10,... | collective-permute-start | bytes 196616 | tf_op jit(solution)/shard_map/ppermute | solution.py:163
  13.0 5.0 %collective-permute-start.4 = (bf16[256,256]{1,0:T(8,128)(2,1)S(1)}, bf16[256,256]{1,0:T(8,128)(2,1)S(1)}, u32[]{:S(2)}, u32[]{:S(2)}) collective-permute-start(bf16[256,256]{1,0:T(8,128)(2,1)S(1)} %constant_dynamic-update-slice_fusion), channel_id=1, source_target_pairs={{0,2},{1,3},{2,0},{3,1},{4,6},{5,7},{6,4},{7,5},{8,10},{9,11},{10,... | collective-permute-start | bytes 393224 | tf_op jit(solution)/shard_map/ppermute | solution.py:163
  13.5 7.7 %collective-permute-start.7 = (bf16[512,256]{1,0:T(8,128)(2,1)S(1)}, bf16[512,256]{1,0:T(8,128)(2,1)S(1)}, u32[]{:S(2)}, u32[]{:S(2)}) collective-permute-start(bf16[512,256]{1,0:T(8,128)(2,1)S(1)} %constant_dynamic-update-slice_fusion.2), channel_id=1, source_target_pairs={{0,1},{1,0},{2,3},{3,2},{4,5},{5,4},{6,7},{7,6},{8,9},{9,8},{10,11... | collective-permute-start | bytes 786440 | tf_op jit(solution)/shard_map/ppermute | solution.py:163
  13.6 4.5 %collective-permute-start.1 = (bf16[128,256]{1,0:T(8,128)(2,1)S(1)}, bf16[128,256]{1,0:T(8,128)(2,1)S(1)}, u32[]{:S(2)}, u32[]{:S(2)}) collective-permute-start(bf16[128,256]{1,0:T(8,128)(2,1)S(1)} %collective-permute-done.refs_1_), channel_id=1, source_target_pairs={{0,4},{1,5},{2,6},{3,7},{4,0},{5,1},{6,2},{7,3},{8,12},{9,13},{10,... | collective-permute-start | bytes 196616 | tf_op jit(solution)/shard_map/ppermute | solution.py:163
  18.1 4.6 %collective-permute-start.6 = (bf16[384,256]{1,0:T(8,128)(2,1)S(1)}, bf16[384,256]{1,0:T(8,128)(2,1)S(1)}, u32[]{:S(2)}, u32[]{:S(2)}) collective-permute-start(bf16[384,256]{1,0:T(8,128)(2,1)S(1)} %pad_maximum_fusion), channel_id=1, source_target_pairs={{0,1},{1,0},{2,3},{3,2},{4,5},{5,4},{6,7},{7,6},{8,9},{9,8},{10,11... | collective-permute-start | bytes 589832 | tf_op jit(solution)/shard_map/ppermute | solution.py:163
  18.2 1.5 %collective-permute-start.8 = (bf16[128,256]{1,0:T(8,128)(2,1)S(1)}, bf16[128,256]{1,0:T(8,128)(2,1)S(1)}, u32[]{:S(2)}, u32[]{:S(2)}) collective-permute-start(bf16[128,256]{1,0:T(8,128)(2,1)S(1)} %get-tuple-element.21.refs_1_), channel_id=1, source_target_pairs={{0,1},{1,0},{2,3},{3,2},{4,5},{5,4},{6,7},{7,6},{8,9},{9,8},{10,11... | collective-permute-start | bytes 196616 | tf_op jit(solution)/shard_map/ppermute | solution.py:163

commit v4 on v3

--- a/solution.py
+++ b/solution.py
@@ -15,13 +15,16 @@
     ("hop", 2, (0,)),
     ("hop", 1, (0,)),
     ("hop", 4, (0,)),
+    ("load", ()),
     ("hop", 4, (2,)),
     ("hop", 2, (8, 12)),
     ("attend", (0, 1)),
-    ("hop", 1, (2, 4, 8, 12)),
+    ("hop", 1, (2, 4, 8)),
     ("attend", (2, 4, 8, 12)),
-    ("hop", 1, (6, 10, 14)),
-    ("attend", (3, 5, 9, 13, 6, 10, 14)),
+    ("hop", 1, (12, 6)),
+    ("attend", (3, 5, 9)),
+    ("hop", 1, (10, 14)),
+    ("attend", (6, 10, 14, 7, 13)),
 )
 
 
@@ -69,28 +72,28 @@
 
 
 def load(*arrays):
-    keys, _, queries = arrays
-    rows, head_size = keys.shape
+    rows = arrays[0].shape[0]
+    width = sum(x.shape[1] for x in arrays)
 
-    def kernel(key_ref, value_ref, query_ref, own_ref, queries_out, sems):
-        copies = [
-            pltpu.make_async_copy(key_ref, own_ref.at[:, pl.ds(0, head_size)], sems.at[0]),
-            pltpu.make_async_copy(value_ref, own_ref.at[:, pl.ds(head_size, head_size)], sems.at[1]),
-            pltpu.make_async_copy(query_ref, queries_out, sems.at[2]),
-        ]
+    def kernel(*refs):
+        *sources, out_ref, sems = refs
+        copies = []
+        at = 0
+        for i, source in enumerate(sources):
+            window = out_ref.at[:, pl.ds(at, source.shape[1])] if len(sources) > 1 else out_ref
+            copies.append(pltpu.make_async_copy(source, window, sems.at[i]))
+            at += source.shape[1]
         for copy in copies:
             copy.start()
         for copy in copies:
             copy.wait()
 
-    whole = pl.BlockSpec(memory_space=pltpu.HBM)
-    vmem = pl.BlockSpec(memory_space=pltpu.VMEM)
     return pl.pallas_call(
         kernel,
-        out_shape=(pltpu.VMEM((rows, 2 * head_size), keys.dtype), pltpu.VMEM(queries.shape, queries.dtype)),
-        in_specs=[whole] * 3,
-        out_specs=(vmem, vmem),
-        scratch_shapes=[pltpu.SemaphoreType.DMA((3,))],
+        out_shape=pltpu.VMEM((rows, width), arrays[0].dtype),
+        in_specs=[pl.BlockSpec(memory_space=pltpu.HBM)] * len(arrays),
+        out_specs=pl.BlockSpec(memory_space=pltpu.VMEM),
+        scratch_shapes=[pltpu.SemaphoreType.DMA((len(arrays),))],
         compiler_params=pltpu.CompilerParams(vmem_limit_bytes=4 << 20),
     )(*[in_hbm(x) for x in arrays])
 
@@ -154,8 +157,13 @@
             for m in held:
                 at, array = known[m]
                 parts.append(array if array.shape[0] == rows else array[at * rows : (at + 1) * rows])
+            arrays = [known[m][1] for m in held]
             if len(parts) == 1:
                 source = parts[0]
+            elif [known[m][0] for m in held] == list(range(arrays[0].shape[0] // rows)) and all(
+                array is arrays[0] for array in arrays
+            ):
+                source = arrays[0]
             else:
                 if joined is not None:
                     parts, joined = lax.optimization_barrier((parts, joined))
@@ -164,6 +172,8 @@
             for at, m in enumerate(held):
                 known[m ^ mask] = (at, got)
             fresh[held[0] ^ mask] = got
+        elif kind == "load":
+            queries = load(queries)
         else:
             units = [fresh.pop(m) for m in what[0] if m in fresh]
             state = attend(queries, units, state)
@@ -174,10 +184,10 @@
     size = mesh.shape["col"]
 
     def per_device(queries, keys, values, out_weight):
-        own, queries = load(keys, values, queries)
+        own = load(keys, values)
         if size % 16:
             own = lax.all_gather(own, "col", axis=0, tiled=True)
-            return project(attend(queries, [own], None, True), out_weight)
+            return project(attend(load(queries), [own], None, True), out_weight)
         return project(run_plan(own, queries, size), out_weight)
 
     spec = P(("groups", "col"), None)

time: 25.9 us -> 25.5 us (0.985)
  waiting for transfers between devices: 9.68 us -> 6.96 us
  starting transfers between devices: 8.8 us -> 10.1 us
  Pallas kernels: 5.04 us -> 6.07 us
    ppermute x9 -> x10, waiting for transfers between devices: 9.68 us -> 6.96 us  [run_plan(): got = lax.ppermute(source, 'col', [(j, j ^ mask) for j in range(size)])]
    ppermute x9 -> x10, starting transfers between devices: 8.8 us -> 10.1 us  [run_plan(): got = lax.ppermute(source, 'col', [(j, j ^ mask) for j in range(size)])]
    pallas_call x1 -> x2, Pallas kernels: 1.15 us -> 1.89 us  [load(): pl.pallas_call(kernel, out_shape=pltpu.VMEM((rows, width), arrays[0].dtyp...]
    pallas_call x4 -> x5, Pallas kernels: 3.89 us -> 4.18 us  [attend(): pl.pallas_call(kernel, out_shape=out_shape, in_specs=[vmem] * len(args),...]
  transfers between devices with their start and end apart: 9 -> 10, of which waited for: 5 -> 4; matrix products, arithmetic and copies ran while one was open for 0% -> 0% of each run, Pallas kernels for 12% -> 18%
where the time goes in v4:
time: 25.5 us; the launch traced here: 25.4 us
  starting transfers between devices  10.1 us (40%)
  waiting for transfers between devices  6.96 us (27%)
  Pallas kernels  6.07 us (24%)
  matrix products  2.05 us (8%)
    ppermute x10, starting transfers between devices, run_plan(): got = lax.ppermute(source, 'col', [(j, j ^ mask) for j in range(size)])  10.1 us
    ppermute x10, waiting for transfers between devices, run_plan(): got = lax.ppermute(source, 'col', [(j, j ^ mask) for j in range(size)])  6.96 us
    pallas_call x5, Pallas kernels, attend(): pl.pallas_call(kernel, out_shape=out_shape, in_specs=[vmem] * len(args),...  4.18 us
    dot_general x1, matrix products, project(): jnp.dot(attended, out_weight, preferred_element_type=jnp.float32)  2.05 us
    pallas_call x2, Pallas kernels, load(): pl.pallas_call(kernel, out_shape=pltpu.VMEM((rows, width), arrays[0].dtyp...  1.89 us
  transfers between devices with their start and end apart: 10, of which 4 were waited for; matrix products, arithmetic and copies ran while one was open for 0% of the time, Pallas kernels for 18%

profile of v4, /device:TPU:0, one launch (start us, length us, event | category | flops | bytes accessed | tf_op | source)
XLA Modules:
  0.0 25.4 jit_solution(16208301896153131735)
XLA Ops:
  0.0 0.0 copy-start
  0.0 0.9 %shard_map.47.refs_1_ = bf16[128,256]{1,0:T(8,128)(2,1)S(1)} custom-call(bf16[128,128]{1,0:T(8,128)(2,1)} %refs_0_.3, bf16[128,128]{1,0:T(8,128)(2,1)} %refs_1_.1), custom_call_target="tpu_custom_call" | custom-call | tf_op jit(solution)/shard_map/pallas_call | solution.py:91
  1.0 4.1 %collective-permute-start = (bf16[128,256]{1,0:T(8,128)(2,1)S(1)}, bf16[128,256]{1,0:T(8,128)(2,1)S(1)}, u32[]{:S(2)}, u32[]{:S(2)}) collective-permute-start(bf16[128,256]{1,0:T(8,128)(2,1)S(1)} %shard_map.47.refs_1_), channel_id=1, source_target_pairs={{0,8},{1,9},{2,10},{3,11},{4,12},{5,13},{6,14},{7,15},{8,0},{9,1},... | collective-permute-start | bytes 196616 | tf_op jit(solution)/shard_map/ppermute | solution.py:171
  5.1 1.3 %collective-permute-start.1 = (bf16[128,256]{1,0:T(8,128)(2,1)S(1)}, bf16[128,256]{1,0:T(8,128)(2,1)S(1)}, u32[]{:S(2)}, u32[]{:S(2)}) collective-permute-start(bf16[128,256]{1,0:T(8,128)(2,1)S(1)} %shard_map.47.refs_1_), channel_id=1, source_target_pairs={{0,12},{1,13},{2,14},{3,15},{4,8},{5,9},{6,10},{7,11},{8,4},{9,5},... | collective-permute-start | bytes 196616 | tf_op jit(solution)/shard_map/ppermute | solution.py:171
  6.4 1.5 %collective-permute-start.4 = (bf16[128,256]{1,0:T(8,128)(2,1)S(1)}, bf16[128,256]{1,0:T(8,128)(2,1)S(1)}, u32[]{:S(2)}, u32[]{:S(2)}) collective-permute-start(bf16[128,256]{1,0:T(8,128)(2,1)S(1)} %shard_map.47.refs_1_), channel_id=1, source_target_pairs={{0,2},{1,3},{2,0},{3,1},{4,6},{5,7},{6,4},{7,5},{8,10},{9,11},{10,... | collective-permute-start | bytes 196616 | tf_op jit(solution)/shard_map/ppermute | solution.py:171
  8.0 0.2 collective-permute-start.6
  8.2 0.6 %collective-permute-done.refs_3_ = bf16[128,256]{1,0:T(8,128)(2,1)S(1)} collective-permute-done((bf16[128,256]{1,0:T(8,128)(2,1)S(1)}, bf16[128,256]{1,0:T(8,128)(2,1)S(1)}, u32[]{:S(2)}, u32[]{:S(2)}) %collective-permute-start) | collective-permute-done | bytes 65568 | tf_op jit(solution)/shard_map/ppermute | solution.py:171
  8.8 2.8 %collective-permute-done.1.refs_4_ = bf16[128,256]{1,0:T(8,128)(2,1)S(1)} collective-permute-done((bf16[128,256]{1,0:T(8,128)(2,1)S(1)}, bf16[128,256]{1,0:T(8,128)(2,1)S(1)}, u32[]{:S(2)}, u32[]{:S(2)}) %collective-permute-start.1) | collective-permute-done | bytes 65568 | tf_op jit(solution)/shard_map/ppermute | solution.py:171
  11.6 1.2 %collective-permute-start.2 = (bf16[256,256]{1,0:T(8,128)(2,1)S(1)}, bf16[256,256]{1,0:T(8,128)(2,1)S(1)}, u32[]{:S(2)}, u32[]{:S(2)}) collective-permute-start(bf16[256,256]{1,0:T(8,128)(2,1)S(1)} %constant_dynamic-update-slice_fusion), channel_id=1, source_target_pairs={{0,2},{1,3},{2,0},{3,1},{4,6},{5,7},{6,4},{7,5},{8,10},{9,11},{10,... | collective-permute-start | bytes 393224 | tf_op jit(solution)/shard_map/ppermute | solution.py:171
  12.9 0.0 collective-permute-done.4.refs_1_
  12.9 0.0 collective-permute-done.6.refs_2_
  12.9 1.0 %collective-permute-start.5 = (bf16[128,256]{1,0:T(8,128)(2,1)S(1)}, bf16[128,256]{1,0:T(8,128)(2,1)S(1)}, u32[]{:S(2)}, u32[]{:S(2)}) collective-permute-start(bf16[128,256]{1,0:T(8,128)(2,1)S(1)} %collective-permute-done.4.refs_1_), channel_id=1, source_target_pairs={{0,4},{1,5},{2,6},{3,7},{4,0},{5,1},{6,2},{7,3},{8,12},{9,13},{10,... | collective-permute-start | bytes 196616 | tf_op jit(solution)/shard_map/ppermute | solution.py:171
  13.9 0.0 collective-permute-start.8
  13.9 3.3 %collective-permute-done.5.refs_1_ = bf16[128,256]{1,0:T(8,128)(2,1)S(1)} collective-permute-done((bf16[128,256]{1,0:T(8,128)(2,1)S(1)}, bf16[128,256]{1,0:T(8,128)(2,1)S(1)}, u32[]{:S(2)}, u32[]{:S(2)}) %collective-permute-start.5) | collective-permute-done | bytes 65568 | tf_op jit(solution)/shard_map/ppermute | solution.py:171
  17.3 0.1 collective-permute-start.7
  17.3 0.0 collective-permute-done.2.refs_2_
  17.3 0.5 %collective-permute-start.3 = (bf16[256,256]{1,0:T(8,128)(2,1)S(1)}, bf16[256,256]{1,0:T(8,128)(2,1)S(1)}, u32[]{:S(2)}, u32[]{:S(2)}) collective-permute-start(bf16[256,256]{1,0:T(8,128)(2,1)S(1)} %collective-permute-done.2.refs_2_), channel_id=1, source_target_pairs={{0,1},{1,0},{2,3},{3,2},{4,5},{5,4},{6,7},{7,6},{8,9},{9,8},{10,11... | collective-permute-start | bytes 393224 | tf_op jit(solution)/shard_map/ppermute | solution.py:171
  17.8 0.1 collective-permute-start.9
  17.9 0.9 %shard_map.46.refs_0_ = bf16[128,896]{1,0:T(8,128)(2,1)S(1)} custom-call(bf16[128,896]{1,0:T(8,128)(2,1)} %refs_0_.2), custom_call_target="tpu_custom_call" | custom-call | tf_op jit(solution)/shard_map/pallas_call | solution.py:91
  18.9 0.2 collective-permute-done.9.refs_2_
  19.1 0.6 %shard_map.48 = (f32[896,128]{1,0:T(8,128)S(1)}, f32[896,256]{1,0:T(8,128)S(1)}) custom-call(bf16[128,896]{1,0:T(8,128)(2,1)S(1)} %shard_map.46.refs_0_, bf16[128,256]{1,0:T(8,128)(2,1)S(1)} %shard_map.47.refs_1_, bf16[128,256]{1,0:T(8,128)(2,1)S(1)} %collective-permute-done.9.refs_2_), custom_call_target="tpu_custom_call" | custom-call | tf_op jit(solution)/shard_map/pallas_call | solution.py:131
  19.7 0.9 %shard_map.49 = (f32[896,128]{1,0:T(8,128)S(1)}, f32[896,256]{1,0:T(8,128)S(1)}) custom-call(bf16[128,896]{1,0:T(8,128)(2,1)S(1)} %shard_map.46.refs_0_, bf16[128,256]{1,0:T(8,128)(2,1)S(1)} %collective-permute-done.4.refs_1_, bf16[128,256]{1,0:T(8,128)(2,1)S(1)} %collective-permute-done.6.refs_2_, bf16[128,256]{1,0:T(8,128)(2,1)S(1)} %collective-permute-done.refs_3_, ...), custom_call_target="tpu_custom_call" | custom-call | tf_op jit(solution)/shard_map/pallas_call | solution.py:131
  20.6 0.0 collective-permute-done.8.refs_1_
  20.6 0.9 %shard_map.50 = (f32[896,128]{1,0:T(8,128)S(1)}, f32[896,256]{1,0:T(8,128)S(1)}) custom-call(bf16[128,896]{1,0:T(8,128)(2,1)S(1)} %shard_map.46.refs_0_, bf16[384,256]{1,0:T(8,128)(2,1)S(1)} %collective-permute-done.8.refs_1_, f32[896,128]{1,0:T(8,128)S(1)} %get-tuple-element.25.refs_2_, f32[896,256]{1,0:T(8,128)S(1)} %get-tuple-element.26.refs_3_), custom_call_target="tpu_custom_call" | custom-call | tf_op jit(solution)/shard_map/pallas_call | solution.py:131
  21.5 0.0 collective-permute-done.7.refs_3_
  21.5 1.2 %shard_map.51 = (f32[896,128]{1,0:T(8,128)S(1)}, f32[896,256]{1,0:T(8,128)S(1)}) custom-call(bf16[128,896]{1,0:T(8,128)(2,1)S(1)} %shard_map.46.refs_0_, bf16[128,256]{1,0:T(8,128)(2,1)S(1)} %collective-permute-done.5.refs_1_, bf16[256,256]{1,0:T(8,128)(2,1)S(1)} %collective-permute-done.2.refs_2_, bf16[256,256]{1,0:T(8,128)(2,1)S(1)} %collective-permute-done.7.refs_3_, ...), custom_call_target="tpu_custom_call" | custom-call | tf_op jit(solution)/shard_map/pallas_call | solution.py:131
  22.7 0.0 collective-permute-done.3.refs_1_
  22.7 0.6 %shard_map.52 = bf16[128,896]{1,0:T(8,128)(2,1)S(1)} custom-call(bf16[128,896]{1,0:T(8,128)(2,1)S(1)} %shard_map.46.refs_0_, bf16[256,256]{1,0:T(8,128)(2,1)S(1)} %collective-permute-done.3.refs_1_, f32[896,128]{1,0:T(8,128)S(1)} %get-tuple-element.29.refs_2_, f32[896,256]{1,0:T(8,128)S(1)} %get-tuple-element.30.refs_3_), custom_call_target="tpu_custom_call" | custom-call | tf_op jit(solution)/shard_map/pallas_call | solution.py:131
  23.3 0.0 copy-done
  23.3 2.0 %convolution_convert_fusion = bf16[128,3584]{1,0:T(8,128)(2,1)} fusion(bf16[128,896]{1,0:T(8,128)(2,1)S(1)} %shard_map.52, bf16[896,3584]{1,0:T(8,128)(2,1)S(1)} %copy-done), kind=kOutput, calls=%fused_computation | convolution fusion | flops 822542336 | bytes 7569408 | tf_op jit(solution)/shard_map/dot_general | solution.py:141
  (6 shorter events, 0.0 us)
Async XLA Ops:
  0.0 23.3 %copy-start = (bf16[896,3584]{1,0:T(8,128)(2,1)S(1)}, bf16[896,3584]{1,0:T(8,128)(2,1)}, u32[]{:S(2)}) copy-start(bf16[896,3584]{1,0:T(8,128)(2,1)} %param.7) | copy-start | bytes 19267588
  1.0 7.8 %collective-permute-start = (bf16[128,256]{1,0:T(8,128)(2,1)S(1)}, bf16[128,256]{1,0:T(8,128)(2,1)S(1)}, u32[]{:S(2)}, u32[]{:S(2)}) collective-permute-start(bf16[128,256]{1,0:T(8,128)(2,1)S(1)} %shard_map.47.refs_1_), channel_id=1, source_target_pairs={{0,8},{1,9},{2,10},{3,11},{4,12},{5,13},{6,14},{7,15},{8,0},{9,1},... | collective-permute-start | bytes 196616 | tf_op jit(solution)/shard_map/ppermute | solution.py:171
  5.1 6.5 %collective-permute-start.1 = (bf16[128,256]{1,0:T(8,128)(2,1)S(1)}, bf16[128,256]{1,0:T(8,128)(2,1)S(1)}, u32[]{:S(2)}, u32[]{:S(2)}) collective-permute-start(bf16[128,256]{1,0:T(8,128)(2,1)S(1)} %shard_map.47.refs_1_), channel_id=1, source_target_pairs={{0,12},{1,13},{2,14},{3,15},{4,8},{5,9},{6,10},{7,11},{8,4},{9,5},... | collective-permute-start | bytes 196616 | tf_op jit(solution)/shard_map/ppermute | solution.py:171
  6.4 6.4 %collective-permute-start.4 = (bf16[128,256]{1,0:T(8,128)(2,1)S(1)}, bf16[128,256]{1,0:T(8,128)(2,1)S(1)}, u32[]{:S(2)}, u32[]{:S(2)}) collective-permute-start(bf16[128,256]{1,0:T(8,128)(2,1)S(1)} %shard_map.47.refs_1_), channel_id=1, source_target_pairs={{0,2},{1,3},{2,0},{3,1},{4,6},{5,7},{6,4},{7,5},{8,10},{9,11},{10,... | collective-permute-start | bytes 196616 | tf_op jit(solution)/shard_map/ppermute | solution.py:171
  8.0 4.9 %collective-permute-start.6 = (bf16[128,256]{1,0:T(8,128)(2,1)S(1)}, bf16[128,256]{1,0:T(8,128)(2,1)S(1)}, u32[]{:S(2)}, u32[]{:S(2)}) collective-permute-start(bf16[128,256]{1,0:T(8,128)(2,1)S(1)} %shard_map.47.refs_1_), channel_id=1, source_target_pairs={{0,4},{1,5},{2,6},{3,7},{4,0},{5,1},{6,2},{7,3},{8,12},{9,13},{10,... | collective-permute-start | bytes 196616 | tf_op jit(solution)/shard_map/ppermute | solution.py:171
  11.6 5.7 %collective-permute-start.2 = (bf16[256,256]{1,0:T(8,128)(2,1)S(1)}, bf16[256,256]{1,0:T(8,128)(2,1)S(1)}, u32[]{:S(2)}, u32[]{:S(2)}) collective-permute-start(bf16[256,256]{1,0:T(8,128)(2,1)S(1)} %constant_dynamic-update-slice_fusion), channel_id=1, source_target_pairs={{0,2},{1,3},{2,0},{3,1},{4,6},{5,7},{6,4},{7,5},{8,10},{9,11},{10,... | collective-permute-start | bytes 393224 | tf_op jit(solution)/shard_map/ppermute | solution.py:171
  12.9 4.3 %collective-permute-start.5 = (bf16[128,256]{1,0:T(8,128)(2,1)S(1)}, bf16[128,256]{1,0:T(8,128)(2,1)S(1)}, u32[]{:S(2)}, u32[]{:S(2)}) collective-permute-start(bf16[128,256]{1,0:T(8,128)(2,1)S(1)} %collective-permute-done.4.refs_1_), channel_id=1, source_target_pairs={{0,4},{1,5},{2,6},{3,7},{4,0},{5,1},{6,2},{7,3},{8,12},{9,13},{10,... | collective-permute-start | bytes 196616 | tf_op jit(solution)/shard_map/ppermute | solution.py:171
  13.9 6.6 %collective-permute-start.8 = (bf16[384,256]{1,0:T(8,128)(2,1)S(1)}, bf16[384,256]{1,0:T(8,128)(2,1)S(1)}, u32[]{:S(2)}, u32[]{:S(2)}) collective-permute-start(bf16[384,256]{1,0:T(8,128)(2,1)S(1)} %constant_dynamic-update-slice_fusion.2), channel_id=1, source_target_pairs={{0,1},{1,0},{2,3},{3,2},{4,5},{5,4},{6,7},{7,6},{8,9},{9,8},{10,11... | collective-permute-start | bytes 589832 | tf_op jit(solution)/shard_map/ppermute | solution.py:171
  17.3 4.2 %collective-permute-start.7 = (bf16[256,256]{1,0:T(8,128)(2,1)S(1)}, bf16[256,256]{1,0:T(8,128)(2,1)S(1)}, u32[]{:S(2)}, u32[]{:S(2)}) collective-permute-start(bf16[256,256]{1,0:T(8,128)(2,1)S(1)} %pad_maximum_fusion), channel_id=1, source_target_pairs={{0,1},{1,0},{2,3},{3,2},{4,5},{5,4},{6,7},{7,6},{8,9},{9,8},{10,11... | collective-permute-start | bytes 393224 | tf_op jit(solution)/shard_map/ppermute | solution.py:171
  17.3 5.4 %collective-permute-start.3 = (bf16[256,256]{1,0:T(8,128)(2,1)S(1)}, bf16[256,256]{1,0:T(8,128)(2,1)S(1)}, u32[]{:S(2)}, u32[]{:S(2)}) collective-permute-start(bf16[256,256]{1,0:T(8,128)(2,1)S(1)} %collective-permute-done.2.refs_2_), channel_id=1, source_target_pairs={{0,1},{1,0},{2,3},{3,2},{4,5},{5,4},{6,7},{7,6},{8,9},{9,8},{10,11... | collective-permute-start | bytes 393224 | tf_op jit(solution)/shard_map/ppermute | solution.py:171
  17.8 1.3 %collective-permute-start.9 = (bf16[128,256]{1,0:T(8,128)(2,1)S(1)}, bf16[128,256]{1,0:T(8,128)(2,1)S(1)}, u32[]{:S(2)}, u32[]{:S(2)}) collective-permute-start(bf16[128,256]{1,0:T(8,128)(2,1)S(1)} %shard_map.47.refs_1_), channel_id=1, source_target_pairs={{0,1},{1,0},{2,3},{3,2},{4,5},{5,4},{6,7},{7,6},{8,9},{9,8},{10,11... | collective-permute-start | bytes 196616 | tf_op jit(solution)/shard_map/ppermute | solution.py:171

commit v5 on v3

--- a/solution.py
+++ b/solution.py
@@ -17,11 +17,12 @@
     ("hop", 4, (0,)),
     ("hop", 4, (2,)),
     ("hop", 2, (8, 12)),
-    ("attend", (0, 1)),
     ("hop", 1, (2, 4, 8, 12)),
-    ("attend", (2, 4, 8, 12)),
-    ("hop", 1, (6, 10, 14)),
-    ("attend", (3, 5, 9, 13, 6, 10, 14)),
+    ("attend", (0, 1, 2, 4, 8, 12)),
+    ("hop", 1, (6,)),
+    ("attend", (3, 5, 9, 13)),
+    ("hop", 1, (10, 14)),
+    ("attend", (6, 10, 14, 7)),
 )
 
 
@@ -71,13 +72,16 @@
 def load(*arrays):
     keys, _, queries = arrays
     rows, head_size = keys.shape
+    pieces = math.gcd(rows // 16, 8)
 
     def kernel(key_ref, value_ref, query_ref, own_ref, queries_out, sems):
         copies = [
             pltpu.make_async_copy(key_ref, own_ref.at[:, pl.ds(0, head_size)], sems.at[0]),
             pltpu.make_async_copy(value_ref, own_ref.at[:, pl.ds(head_size, head_size)], sems.at[1]),
-            pltpu.make_async_copy(query_ref, queries_out, sems.at[2]),
         ]
+        for i in range(pieces):
+            at = pl.ds(i * (rows // pieces), rows // pieces)
+            copies.append(pltpu.make_async_copy(query_ref.at[at], queries_out.at[at], sems.at[2 + i]))
         for copy in copies:
             copy.start()
         for copy in copies:
@@ -90,7 +94,7 @@
         out_shape=(pltpu.VMEM((rows, 2 * head_size), keys.dtype), pltpu.VMEM(queries.shape, queries.dtype)),
         in_specs=[whole] * 3,
         out_specs=(vmem, vmem),
-        scratch_shapes=[pltpu.SemaphoreType.DMA((3,))],
+        scratch_shapes=[pltpu.SemaphoreType.DMA((2 + pieces,))],
         compiler_params=pltpu.CompilerParams(vmem_limit_bytes=4 << 20),
     )(*[in_hbm(x) for x in arrays])
 
@@ -154,8 +158,13 @@
             for m in held:
                 at, array = known[m]
                 parts.append(array if array.shape[0] == rows else array[at * rows : (at + 1) * rows])
+            arrays = [known[m][1] for m in held]
             if len(parts) == 1:
                 source = parts[0]
+            elif [known[m][0] for m in held] == list(range(arrays[0].shape[0] // rows)) and all(
+                array is arrays[0] for array in arrays
+            ):
+                source = arrays[0]
             else:
                 if joined is not None:
                     parts, joined = lax.optimization_barrier((parts, joined))

time: 25.9 us -> 25.7 us (level)
  starting transfers between devices: 8.8 us -> 9.47 us
  waiting for transfers between devices: 9.68 us -> 9.25 us
  Pallas kernels: 5.04 us -> 4.65 us
    ppermute x9 -> x10, starting transfers between devices: 8.8 us -> 9.47 us  [run_plan(): got = lax.ppermute(source, 'col', [(j, j ^ mask) for j in range(size)])]
    ppermute x9 -> x10, waiting for transfers between devices: 9.68 us -> 9.25 us  [run_plan(): got = lax.ppermute(source, 'col', [(j, j ^ mask) for j in range(size)])]
    pallas_call x4, Pallas kernels: 3.89 us -> 3.53 us  [attend(): pl.pallas_call(kernel, out_shape=out_shape, in_specs=[vmem] * len(args),...]
  transfers between devices with their start and end apart: 9 -> 10, of which waited for: 5 -> 5; matrix products, arithmetic and copies ran while one was open for 0% -> 0% of each run, Pallas kernels for 12% -> 11%
where the time goes in v5:
time: 25.7 us; the launch traced here: 25.5 us
  starting transfers between devices  9.47 us (37%)
  waiting for transfers between devices  9.25 us (36%)
  Pallas kernels  4.65 us (18%)
  matrix products  2.06 us (8%)
    ppermute x10, starting transfers between devices, run_plan(): got = lax.ppermute(source, 'col', [(j, j ^ mask) for j in range(size)])  9.47 us
    ppermute x10, waiting for transfers between devices, run_plan(): got = lax.ppermute(source, 'col', [(j, j ^ mask) for j in range(size)])  9.25 us
    pallas_call x4, Pallas kernels, attend(): pl.pallas_call(kernel, out_shape=out_shape, in_specs=[vmem] * len(args),...  3.53 us
    dot_general x1, matrix products, project(): jnp.dot(attended, out_weight, preferred_element_type=jnp.float32)  2.06 us
    pallas_call x1, Pallas kernels, load(): pl.pallas_call(kernel, out_shape=(pltpu.VMEM((rows, 2 * head_size), keys....  1.12 us
  transfers between devices with their start and end apart: 10, of which 5 were waited for; matrix products, arithmetic and copies ran while one was open for 0% of the time, Pallas kernels for 11%

profile of v5, /device:TPU:0, one launch (start us, length us, event | category | flops | bytes accessed | tf_op | source)
XLA Modules:
  0.0 25.5 jit_solution(12586910222309489626)
XLA Ops:
  0.0 0.0 copy-start
  0.0 1.1 %shard_map.46 = (bf16[128,256]{1,0:T(8,128)(2,1)S(1)}, bf16[128,896]{1,0:T(8,128)(2,1)S(1)}) custom-call(bf16[128,128]{1,0:T(8,128)(2,1)} %key_ref.1, bf16[128,128]{1,0:T(8,128)(2,1)} %value_ref.1, bf16[128,896]{1,0:T(8,128)(2,1)} %query_ref.1), custom_call_target="tpu_custom_call" | custom-call | tf_op jit(solution)/shard_map/pallas_call | solution.py:92
  1.1 4.1 %collective-permute-start = (bf16[128,256]{1,0:T(8,128)(2,1)S(1)}, bf16[128,256]{1,0:T(8,128)(2,1)S(1)}, u32[]{:S(2)}, u32[]{:S(2)}) collective-permute-start(bf16[128,256]{1,0:T(8,128)(2,1)S(1)} %get-tuple-element.18.refs_1_), channel_id=1, source_target_pairs={{0,8},{1,9},{2,10},{3,11},{4,12},{5,13},{6,14},{7,15},{8,0},{9,1},... | collective-permute-start | bytes 196616 | tf_op jit(solution)/shard_map/ppermute | solution.py:172
  5.3 1.3 %collective-permute-start.1 = (bf16[128,256]{1,0:T(8,128)(2,1)S(1)}, bf16[128,256]{1,0:T(8,128)(2,1)S(1)}, u32[]{:S(2)}, u32[]{:S(2)}) collective-permute-start(bf16[128,256]{1,0:T(8,128)(2,1)S(1)} %get-tuple-element.18.refs_1_), channel_id=1, source_target_pairs={{0,12},{1,13},{2,14},{3,15},{4,8},{5,9},{6,10},{7,11},{8,4},{9,5},... | collective-permute-start | bytes 196616 | tf_op jit(solution)/shard_map/ppermute | solution.py:172
  6.6 1.5 %collective-permute-start.4 = (bf16[128,256]{1,0:T(8,128)(2,1)S(1)}, bf16[128,256]{1,0:T(8,128)(2,1)S(1)}, u32[]{:S(2)}, u32[]{:S(2)}) collective-permute-start(bf16[128,256]{1,0:T(8,128)(2,1)S(1)} %get-tuple-element.18.refs_1_), channel_id=1, source_target_pairs={{0,2},{1,3},{2,0},{3,1},{4,6},{5,7},{6,4},{7,5},{8,10},{9,11},{10,... | collective-permute-start | bytes 196616 | tf_op jit(solution)/shard_map/ppermute | solution.py:172
  8.1 0.2 collective-permute-start.7
  8.4 0.6 %collective-permute-done.refs_5_ = bf16[128,256]{1,0:T(8,128)(2,1)S(1)} collective-permute-done((bf16[128,256]{1,0:T(8,128)(2,1)S(1)}, bf16[128,256]{1,0:T(8,128)(2,1)S(1)}, u32[]{:S(2)}, u32[]{:S(2)}) %collective-permute-start) | collective-permute-done | bytes 65568 | tf_op jit(solution)/shard_map/ppermute | solution.py:172
  9.0 2.8 %collective-permute-done.1.refs_6_ = bf16[128,256]{1,0:T(8,128)(2,1)S(1)} collective-permute-done((bf16[128,256]{1,0:T(8,128)(2,1)S(1)}, bf16[128,256]{1,0:T(8,128)(2,1)S(1)}, u32[]{:S(2)}, u32[]{:S(2)}) %collective-permute-start.1) | collective-permute-done | bytes 65568 | tf_op jit(solution)/shard_map/ppermute | solution.py:172
  11.8 0.0 collective-permute-done.4.refs_3_
  11.8 0.6 %collective-permute-done.7.refs_4_ = bf16[128,256]{1,0:T(8,128)(2,1)S(1)} collective-permute-done((bf16[128,256]{1,0:T(8,128)(2,1)S(1)}, bf16[128,256]{1,0:T(8,128)(2,1)S(1)}, u32[]{:S(2)}, u32[]{:S(2)}) %collective-permute-start.7) | collective-permute-done | bytes 65568 | tf_op jit(solution)/shard_map/ppermute | solution.py:172
  12.5 0.1 collective-permute-start.8
  12.6 1.2 %collective-permute-start.2 = (bf16[256,256]{1,0:T(8,128)(2,1)S(1)}, bf16[256,256]{1,0:T(8,128)(2,1)S(1)}, u32[]{:S(2)}, u32[]{:S(2)}) collective-permute-start(bf16[256,256]{1,0:T(8,128)(2,1)S(1)} %constant_dynamic-update-slice_fusion), channel_id=1, source_target_pairs={{0,2},{1,3},{2,0},{3,1},{4,6},{5,7},{6,4},{7,5},{8,10},{9,11},{10,... | collective-permute-start | bytes 393224 | tf_op jit(solution)/shard_map/ppermute | solution.py:172
  13.8 0.4 %collective-permute-start.5 = (bf16[128,256]{1,0:T(8,128)(2,1)S(1)}, bf16[128,256]{1,0:T(8,128)(2,1)S(1)}, u32[]{:S(2)}, u32[]{:S(2)}) collective-permute-start(bf16[128,256]{1,0:T(8,128)(2,1)S(1)} %collective-permute-done.4.refs_3_), channel_id=1, source_target_pairs={{0,4},{1,5},{2,6},{3,7},{4,0},{5,1},{6,2},{7,3},{8,12},{9,13},{10,... | collective-permute-start | bytes 196616 | tf_op jit(solution)/shard_map/ppermute | solution.py:172
  14.2 4.2 %collective-permute-done.2.refs_2_ = bf16[256,256]{1,0:T(8,128)(2,1)S(1)} collective-permute-done((bf16[256,256]{1,0:T(8,128)(2,1)S(1)}, bf16[256,256]{1,0:T(8,128)(2,1)S(1)}, u32[]{:S(2)}, u32[]{:S(2)}) %collective-permute-start.2) | collective-permute-done | bytes 131104 | tf_op jit(solution)/shard_map/ppermute | solution.py:172
  18.5 0.0 collective-permute-start.3
  18.5 0.5 %collective-permute-start.9 = (bf16[128,256]{1,0:T(8,128)(2,1)S(1)}, bf16[128,256]{1,0:T(8,128)(2,1)S(1)}, u32[]{:S(2)}, u32[]{:S(2)}) collective-permute-start(bf16[128,256]{1,0:T(8,128)(2,1)S(1)} %get-tuple-element.18.refs_1_), channel_id=1, source_target_pairs={{0,1},{1,0},{2,3},{3,2},{4,5},{5,4},{6,7},{7,6},{8,9},{9,8},{10,11... | collective-permute-start | bytes 196616 | tf_op jit(solution)/shard_map/ppermute | solution.py:172
  19.0 0.0 collective-permute-done.5.refs_1_
  19.0 0.0 collective-permute-start.6
  19.0 0.9 %collective-permute-done.9.refs_2_ = bf16[128,256]{1,0:T(8,128)(2,1)S(1)} collective-permute-done((bf16[128,256]{1,0:T(8,128)(2,1)S(1)}, bf16[128,256]{1,0:T(8,128)(2,1)S(1)}, u32[]{:S(2)}, u32[]{:S(2)}) %collective-permute-start.9) | collective-permute-done | bytes 65568 | tf_op jit(solution)/shard_map/ppermute | solution.py:172
  19.9 1.2 %shard_map.47 = (f32[896,128]{1,0:T(8,128)S(1)}, f32[896,256]{1,0:T(8,128)S(1)}) custom-call(bf16[128,896]{1,0:T(8,128)(2,1)S(1)} %get-tuple-element.17.refs_0_, bf16[128,256]{1,0:T(8,128)(2,1)S(1)} %get-tuple-element.18.refs_1_, bf16[128,256]{1,0:T(8,128)(2,1)S(1)} %collective-permute-done.9.refs_2_, bf16[128,256]{1,0:T(8,128)(2,1)S(1)} %collective-permute-done.4.refs_3_, ...), custom_call_target="tpu_custom_call" | custom-call | tf_op jit(solution)/shard_map/pallas_call | solution.py:132
  21.1 0.0 collective-permute-done.8.refs_1_
  21.1 0.9 %shard_map.48 = (f32[896,128]{1,0:T(8,128)S(1)}, f32[896,256]{1,0:T(8,128)S(1)}) custom-call(bf16[128,896]{1,0:T(8,128)(2,1)S(1)} %get-tuple-element.17.refs_0_, bf16[512,256]{1,0:T(8,128)(2,1)S(1)} %collective-permute-done.8.refs_1_, f32[896,128]{1,0:T(8,128)S(1)} %get-tuple-element.23.refs_2_, f32[896,256]{1,0:T(8,128)S(1)} %get-tuple-element.24.refs_3_), custom_call_target="tpu_custom_call" | custom-call | tf_op jit(solution)/shard_map/pallas_call | solution.py:132
  22.0 0.0 collective-permute-done.6.refs_3_
  22.0 0.9 %shard_map.49 = (f32[896,128]{1,0:T(8,128)S(1)}, f32[896,256]{1,0:T(8,128)S(1)}) custom-call(bf16[128,896]{1,0:T(8,128)(2,1)S(1)} %get-tuple-element.17.refs_0_, bf16[128,256]{1,0:T(8,128)(2,1)S(1)} %collective-permute-done.5.refs_1_, bf16[256,256]{1,0:T(8,128)(2,1)S(1)} %collective-permute-done.2.refs_2_, ...), custom_call_target="tpu_custom_call" | custom-call | tf_op jit(solution)/shard_map/pallas_call | solution.py:132
  22.9 0.0 collective-permute-done.3.refs_1_
  22.9 0.6 %shard_map.50 = bf16[128,896]{1,0:T(8,128)(2,1)S(1)} custom-call(bf16[128,896]{1,0:T(8,128)(2,1)S(1)} %get-tuple-element.17.refs_0_, bf16[256,256]{1,0:T(8,128)(2,1)S(1)} %collective-permute-done.3.refs_1_, f32[896,128]{1,0:T(8,128)S(1)} %get-tuple-element.27.refs_2_, f32[896,256]{1,0:T(8,128)S(1)} %get-tuple-element.28.refs_3_), custom_call_target="tpu_custom_call" | custom-call | tf_op jit(solution)/shard_map/pallas_call | solution.py:132
  23.5 0.0 copy-done
  23.5 2.1 %convolution_convert_fusion = bf16[128,3584]{1,0:T(8,128)(2,1)} fusion(bf16[128,896]{1,0:T(8,128)(2,1)S(1)} %shard_map.50, bf16[896,3584]{1,0:T(8,128)(2,1)S(1)} %copy-done), kind=kOutput, calls=%fused_computation | convolution fusion | flops 822542336 | bytes 7569408 | tf_op jit(solution)/shard_map/dot_general | solution.py:142
  (3 shorter events, 0.0 us)
Async XLA Ops:
  0.0 23.5 %copy-start = (bf16[896,3584]{1,0:T(8,128)(2,1)S(1)}, bf16[896,3584]{1,0:T(8,128)(2,1)}, u32[]{:S(2)}) copy-start(bf16[896,3584]{1,0:T(8,128)(2,1)} %param.7) | copy-start | bytes 19267588
  1.1 7.8 %collective-permute-start = (bf16[128,256]{1,0:T(8,128)(2,1)S(1)}, bf16[128,256]{1,0:T(8,128)(2,1)S(1)}, u32[]{:S(2)}, u32[]{:S(2)}) collective-permute-start(bf16[128,256]{1,0:T(8,128)(2,1)S(1)} %get-tuple-element.18.refs_1_), channel_id=1, source_target_pairs={{0,8},{1,9},{2,10},{3,11},{4,12},{5,13},{6,14},{7,15},{8,0},{9,1},... | collective-permute-start | bytes 196616 | tf_op jit(solution)/shard_map/ppermute | solution.py:172
  5.3 6.5 %collective-permute-start.1 = (bf16[128,256]{1,0:T(8,128)(2,1)S(1)}, bf16[128,256]{1,0:T(8,128)(2,1)S(1)}, u32[]{:S(2)}, u32[]{:S(2)}) collective-permute-start(bf16[128,256]{1,0:T(8,128)(2,1)S(1)} %get-tuple-element.18.refs_1_), channel_id=1, source_target_pairs={{0,12},{1,13},{2,14},{3,15},{4,8},{5,9},{6,10},{7,11},{8,4},{9,5},... | collective-permute-start | bytes 196616 | tf_op jit(solution)/shard_map/ppermute | solution.py:172
  6.6 5.2 %collective-permute-start.4 = (bf16[128,256]{1,0:T(8,128)(2,1)S(1)}, bf16[128,256]{1,0:T(8,128)(2,1)S(1)}, u32[]{:S(2)}, u32[]{:S(2)}) collective-permute-start(bf16[128,256]{1,0:T(8,128)(2,1)S(1)} %get-tuple-element.18.refs_1_), channel_id=1, source_target_pairs={{0,2},{1,3},{2,0},{3,1},{4,6},{5,7},{6,4},{7,5},{8,10},{9,11},{10,... | collective-permute-start | bytes 196616 | tf_op jit(solution)/shard_map/ppermute | solution.py:172
  8.1 4.3 %collective-permute-start.7 = (bf16[128,256]{1,0:T(8,128)(2,1)S(1)}, bf16[128,256]{1,0:T(8,128)(2,1)S(1)}, u32[]{:S(2)}, u32[]{:S(2)}) collective-permute-start(bf16[128,256]{1,0:T(8,128)(2,1)S(1)} %get-tuple-element.18.refs_1_), channel_id=1, source_target_pairs={{0,4},{1,5},{2,6},{3,7},{4,0},{5,1},{6,2},{7,3},{8,12},{9,13},{10,... | collective-permute-start | bytes 196616 | tf_op jit(solution)/shard_map/ppermute | solution.py:172
  12.5 8.6 %collective-permute-start.8 = (bf16[512,256]{1,0:T(8,128)(2,1)S(1)}, bf16[512,256]{1,0:T(8,128)(2,1)S(1)}, u32[]{:S(2)}, u32[]{:S(2)}) collective-permute-start(bf16[512,256]{1,0:T(8,128)(2,1)S(1)} %pad_maximum_fusion), channel_id=1, source_target_pairs={{0,1},{1,0},{2,3},{3,2},{4,5},{5,4},{6,7},{7,6},{8,9},{9,8},{10,11... | collective-permute-start | bytes 786440 | tf_op jit(solution)/shard_map/ppermute | solution.py:172
  12.6 5.9 %collective-permute-start.2 = (bf16[256,256]{1,0:T(8,128)(2,1)S(1)}, bf16[256,256]{1,0:T(8,128)(2,1)S(1)}, u32[]{:S(2)}, u32[]{:S(2)}) collective-permute-start(bf16[256,256]{1,0:T(8,128)(2,1)S(1)} %constant_dynamic-update-slice_fusion), channel_id=1, source_target_pairs={{0,2},{1,3},{2,0},{3,1},{4,6},{5,7},{6,4},{7,5},{8,10},{9,11},{10,... | collective-permute-start | bytes 393224 | tf_op jit(solution)/shard_map/ppermute | solution.py:172
  13.8 5.2 %collective-permute-start.5 = (bf16[128,256]{1,0:T(8,128)(2,1)S(1)}, bf16[128,256]{1,0:T(8,128)(2,1)S(1)}, u32[]{:S(2)}, u32[]{:S(2)}) collective-permute-start(bf16[128,256]{1,0:T(8,128)(2,1)S(1)} %collective-permute-done.4.refs_3_), channel_id=1, source_target_pairs={{0,4},{1,5},{2,6},{3,7},{4,0},{5,1},{6,2},{7,3},{8,12},{9,13},{10,... | collective-permute-start | bytes 196616 | tf_op jit(solution)/shard_map/ppermute | solution.py:172
  18.5 4.4 %collective-permute-start.3 = (bf16[256,256]{1,0:T(8,128)(2,1)S(1)}, bf16[256,256]{1,0:T(8,128)(2,1)S(1)}, u32[]{:S(2)}, u32[]{:S(2)}) collective-permute-start(bf16[256,256]{1,0:T(8,128)(2,1)S(1)} %collective-permute-done.2.refs_2_), channel_id=1, source_target_pairs={{0,1},{1,0},{2,3},{3,2},{4,5},{5,4},{6,7},{7,6},{8,9},{9,8},{10,11... | collective-permute-start | bytes 393224 | tf_op jit(solution)/shard_map/ppermute | solution.py:172
  18.5 1.4 %collective-permute-start.9 = (bf16[128,256]{1,0:T(8,128)(2,1)S(1)}, bf16[128,256]{1,0:T(8,128)(2,1)S(1)}, u32[]{:S(2)}, u32[]{:S(2)}) collective-permute-start(bf16[128,256]{1,0:T(8,128)(2,1)S(1)} %get-tuple-element.18.refs_1_), channel_id=1, source_target_pairs={{0,1},{1,0},{2,3},{3,2},{4,5},{5,4},{6,7},{7,6},{8,9},{9,8},{10,11... | collective-permute-start | bytes 196616 | tf_op jit(solution)/shard_map/ppermute | solution.py:172
  19.0 3.0 %collective-permute-start.6 = (bf16[128,256]{1,0:T(8,128)(2,1)S(1)}, bf16[128,256]{1,0:T(8,128)(2,1)S(1)}, u32[]{:S(2)}, u32[]{:S(2)}) collective-permute-start(bf16[128,256]{1,0:T(8,128)(2,1)S(1)} %collective-permute-done.5.refs_1_), channel_id=1, source_target_pairs={{0,1},{1,0},{2,3},{3,2},{4,5},{5,4},{6,7},{7,6},{8,9},{9,8},{10,11... | collective-permute-start | bytes 196616 | tf_op jit(solution)/shard_map/ppermute | solution.py:172

commit v6 on v4

--- a/solution.py
+++ b/solution.py
@@ -18,13 +18,12 @@
     ("load", ()),
     ("hop", 4, (2,)),
     ("hop", 2, (8, 12)),
-    ("attend", (0, 1)),
-    ("hop", 1, (2, 4, 8)),
-    ("attend", (2, 4, 8, 12)),
-    ("hop", 1, (12, 6)),
-    ("attend", (3, 5, 9)),
+    ("hop", 1, (2, 4, 8, 12)),
+    ("attend", (0, 1, 2, 4, 8, 12)),
+    ("hop", 1, (6,)),
+    ("attend", (3, 5, 9, 13)),
     ("hop", 1, (10, 14)),
-    ("attend", (6, 10, 14, 7, 13)),
+    ("attend", (6, 10, 14, 7)),
 )
 
 

time: 25.5 us -> 25.6 us (level)
  waiting for transfers between devices: 6.96 us -> 8.33 us
  Pallas kernels: 6.07 us -> 5.42 us
  starting transfers between devices: 10.1 us -> 9.47 us
    ppermute x10, waiting for transfers between devices: 6.96 us -> 8.33 us  [run_plan(): got = lax.ppermute(source, 'col', [(j, j ^ mask) for j in range(size)])]
    ppermute x10, starting transfers between devices: 10.1 us -> 9.47 us  [run_plan(): got = lax.ppermute(source, 'col', [(j, j ^ mask) for j in range(size)])]
    pallas_call x5 -> x4, Pallas kernels: 4.18 us -> 3.53 us  [attend(): pl.pallas_call(kernel, out_shape=out_shape, in_specs=[vmem] * len(args),...]
  transfers between devices with their start and end apart: 10 -> 10, of which waited for: 4 -> 4; matrix products, arithmetic and copies ran while one was open for 0% -> 0% of each run, Pallas kernels for 18% -> 15%
where the time goes in v6:
time: 25.6 us; the launch traced here: 25.4 us
  starting transfers between devices  9.47 us (37%)
  waiting for transfers between devices  8.33 us (33%)
  Pallas kernels  5.42 us (21%)
  matrix products  2.05 us (8%)
    ppermute x10, starting transfers between devices, run_plan(): got = lax.ppermute(source, 'col', [(j, j ^ mask) for j in range(size)])  9.47 us
    ppermute x10, waiting for transfers between devices, run_plan(): got = lax.ppermute(source, 'col', [(j, j ^ mask) for j in range(size)])  8.33 us
    pallas_call x4, Pallas kernels, attend(): pl.pallas_call(kernel, out_shape=out_shape, in_specs=[vmem] * len(args),...  3.53 us
    dot_general x1, matrix products, project(): jnp.dot(attended, out_weight, preferred_element_type=jnp.float32)  2.05 us
    pallas_call x2, Pallas kernels, load(): pl.pallas_call(kernel, out_shape=pltpu.VMEM((rows, width), arrays[0].dtyp...  1.89 us
  transfers between devices with their start and end apart: 10, of which 4 were waited for; matrix products, arithmetic and copies ran while one was open for 0% of the time, Pallas kernels for 15%

profile of v6, /device:TPU:0, one launch (start us, length us, event | category | flops | bytes accessed | tf_op | source)
XLA Modules:
  0.0 25.4 jit_solution(5240700960243528173)
XLA Ops:
  0.0 0.0 copy-start
  0.0 0.9 %shard_map.47.refs_1_ = bf16[128,256]{1,0:T(8,128)(2,1)S(1)} custom-call(bf16[128,128]{1,0:T(8,128)(2,1)} %refs_0_.3, bf16[128,128]{1,0:T(8,128)(2,1)} %refs_1_.1), custom_call_target="tpu_custom_call" | custom-call | tf_op jit(solution)/shard_map/pallas_call | solution.py:90
  1.0 4.1 %collective-permute-start = (bf16[128,256]{1,0:T(8,128)(2,1)S(1)}, bf16[128,256]{1,0:T(8,128)(2,1)S(1)}, u32[]{:S(2)}, u32[]{:S(2)}) collective-permute-start(bf16[128,256]{1,0:T(8,128)(2,1)S(1)} %shard_map.47.refs_1_), channel_id=1, source_target_pairs={{0,8},{1,9},{2,10},{3,11},{4,12},{5,13},{6,14},{7,15},{8,0},{9,1},... | collective-permute-start | bytes 196616 | tf_op jit(solution)/shard_map/ppermute | solution.py:170
  5.1 1.3 %collective-permute-start.1 = (bf16[128,256]{1,0:T(8,128)(2,1)S(1)}, bf16[128,256]{1,0:T(8,128)(2,1)S(1)}, u32[]{:S(2)}, u32[]{:S(2)}) collective-permute-start(bf16[128,256]{1,0:T(8,128)(2,1)S(1)} %shard_map.47.refs_1_), channel_id=1, source_target_pairs={{0,12},{1,13},{2,14},{3,15},{4,8},{5,9},{6,10},{7,11},{8,4},{9,5},... | collective-permute-start | bytes 196616 | tf_op jit(solution)/shard_map/ppermute | solution.py:170
  6.4 1.5 %collective-permute-start.4 = (bf16[128,256]{1,0:T(8,128)(2,1)S(1)}, bf16[128,256]{1,0:T(8,128)(2,1)S(1)}, u32[]{:S(2)}, u32[]{:S(2)}) collective-permute-start(bf16[128,256]{1,0:T(8,128)(2,1)S(1)} %shard_map.47.refs_1_), channel_id=1, source_target_pairs={{0,2},{1,3},{2,0},{3,1},{4,6},{5,7},{6,4},{7,5},{8,10},{9,11},{10,... | collective-permute-start | bytes 196616 | tf_op jit(solution)/shard_map/ppermute | solution.py:170
  8.0 0.2 collective-permute-start.7
  8.2 0.6 %collective-permute-done.refs_5_ = bf16[128,256]{1,0:T(8,128)(2,1)S(1)} collective-permute-done((bf16[128,256]{1,0:T(8,128)(2,1)S(1)}, bf16[128,256]{1,0:T(8,128)(2,1)S(1)}, u32[]{:S(2)}, u32[]{:S(2)}) %collective-permute-start) | collective-permute-done | bytes 65568 | tf_op jit(solution)/shard_map/ppermute | solution.py:170
  8.8 2.8 %collective-permute-done.1.refs_6_ = bf16[128,256]{1,0:T(8,128)(2,1)S(1)} collective-permute-done((bf16[128,256]{1,0:T(8,128)(2,1)S(1)}, bf16[128,256]{1,0:T(8,128)(2,1)S(1)}, u32[]{:S(2)}, u32[]{:S(2)}) %collective-permute-start.1) | collective-permute-done | bytes 65568 | tf_op jit(solution)/shard_map/ppermute | solution.py:170
  11.6 0.0 collective-permute-done.4.refs_3_
  11.6 0.6 %collective-permute-done.7.refs_4_ = bf16[128,256]{1,0:T(8,128)(2,1)S(1)} collective-permute-done((bf16[128,256]{1,0:T(8,128)(2,1)S(1)}, bf16[128,256]{1,0:T(8,128)(2,1)S(1)}, u32[]{:S(2)}, u32[]{:S(2)}) %collective-permute-start.7) | collective-permute-done | bytes 65568 | tf_op jit(solution)/shard_map/ppermute | solution.py:170
  12.3 0.1 collective-permute-start.8
  12.4 1.2 %collective-permute-start.2 = (bf16[256,256]{1,0:T(8,128)(2,1)S(1)}, bf16[256,256]{1,0:T(8,128)(2,1)S(1)}, u32[]{:S(2)}, u32[]{:S(2)}) collective-permute-start(bf16[256,256]{1,0:T(8,128)(2,1)S(1)} %constant_dynamic-update-slice_fusion), channel_id=1, source_target_pairs={{0,2},{1,3},{2,0},{3,1},{4,6},{5,7},{6,4},{7,5},{8,10},{9,11},{10,... | collective-permute-start | bytes 393224 | tf_op jit(solution)/shard_map/ppermute | solution.py:170
  13.6 0.4 %collective-permute-start.5 = (bf16[128,256]{1,0:T(8,128)(2,1)S(1)}, bf16[128,256]{1,0:T(8,128)(2,1)S(1)}, u32[]{:S(2)}, u32[]{:S(2)}) collective-permute-start(bf16[128,256]{1,0:T(8,128)(2,1)S(1)} %collective-permute-done.4.refs_3_), channel_id=1, source_target_pairs={{0,4},{1,5},{2,6},{3,7},{4,0},{5,1},{6,2},{7,3},{8,12},{9,13},{10,... | collective-permute-start | bytes 196616 | tf_op jit(solution)/shard_map/ppermute | solution.py:170
  14.0 4.2 %collective-permute-done.2.refs_2_ = bf16[256,256]{1,0:T(8,128)(2,1)S(1)} collective-permute-done((bf16[256,256]{1,0:T(8,128)(2,1)S(1)}, bf16[256,256]{1,0:T(8,128)(2,1)S(1)}, u32[]{:S(2)}, u32[]{:S(2)}) %collective-permute-start.2) | collective-permute-done | bytes 131104 | tf_op jit(solution)/shard_map/ppermute | solution.py:170
  18.3 0.0 collective-permute-start.3
  18.3 0.5 %collective-permute-start.9 = (bf16[128,256]{1,0:T(8,128)(2,1)S(1)}, bf16[128,256]{1,0:T(8,128)(2,1)S(1)}, u32[]{:S(2)}, u32[]{:S(2)}) collective-permute-start(bf16[128,256]{1,0:T(8,128)(2,1)S(1)} %shard_map.47.refs_1_), channel_id=1, source_target_pairs={{0,1},{1,0},{2,3},{3,2},{4,5},{5,4},{6,7},{7,6},{8,9},{9,8},{10,11... | collective-permute-start | bytes 196616 | tf_op jit(solution)/shard_map/ppermute | solution.py:170
  18.8 0.0 collective-permute-done.5.refs_1_
  18.8 0.0 collective-permute-start.6
  18.8 0.9 %shard_map.46.refs_0_ = bf16[128,896]{1,0:T(8,128)(2,1)S(1)} custom-call(bf16[128,896]{1,0:T(8,128)(2,1)} %refs_0_.2), custom_call_target="tpu_custom_call" | custom-call | tf_op jit(solution)/shard_map/pallas_call | solution.py:90
  19.7 0.0 collective-permute-done.9.refs_2_
  19.8 1.2 %shard_map.48 = (f32[896,128]{1,0:T(8,128)S(1)}, f32[896,256]{1,0:T(8,128)S(1)}) custom-call(bf16[128,896]{1,0:T(8,128)(2,1)S(1)} %shard_map.46.refs_0_, bf16[128,256]{1,0:T(8,128)(2,1)S(1)} %shard_map.47.refs_1_, bf16[128,256]{1,0:T(8,128)(2,1)S(1)} %collective-permute-done.9.refs_2_, bf16[128,256]{1,0:T(8,128)(2,1)S(1)} %collective-permute-done.4.refs_3_, ...), custom_call_target="tpu_custom_call" | custom-call | tf_op jit(solution)/shard_map/pallas_call | solution.py:130
  20.9 0.0 collective-permute-done.8.refs_1_
  20.9 0.9 %shard_map.49 = (f32[896,128]{1,0:T(8,128)S(1)}, f32[896,256]{1,0:T(8,128)S(1)}) custom-call(bf16[128,896]{1,0:T(8,128)(2,1)S(1)} %shard_map.46.refs_0_, bf16[512,256]{1,0:T(8,128)(2,1)S(1)} %collective-permute-done.8.refs_1_, f32[896,128]{1,0:T(8,128)S(1)} %get-tuple-element.19.refs_2_, f32[896,256]{1,0:T(8,128)S(1)} %get-tuple-element.20.refs_3_), custom_call_target="tpu_custom_call" | custom-call | tf_op jit(solution)/shard_map/pallas_call | solution.py:130
  21.8 0.0 collective-permute-done.6.refs_3_
  21.8 0.9 %shard_map.50 = (f32[896,128]{1,0:T(8,128)S(1)}, f32[896,256]{1,0:T(8,128)S(1)}) custom-call(bf16[128,896]{1,0:T(8,128)(2,1)S(1)} %shard_map.46.refs_0_, bf16[128,256]{1,0:T(8,128)(2,1)S(1)} %collective-permute-done.5.refs_1_, bf16[256,256]{1,0:T(8,128)(2,1)S(1)} %collective-permute-done.2.refs_2_, bf16[128,256]{1,0:T(8,128)(2,1)S(1)} %collective-permute-done.6.refs_3_, ...), custom_call_target="tpu_custom_call" | custom-call | tf_op jit(solution)/shard_map/pallas_call | solution.py:130
  22.7 0.0 collective-permute-done.3.refs_1_
  22.7 0.6 %shard_map.51 = bf16[128,896]{1,0:T(8,128)(2,1)S(1)} custom-call(bf16[128,896]{1,0:T(8,128)(2,1)S(1)} %shard_map.46.refs_0_, bf16[256,256]{1,0:T(8,128)(2,1)S(1)} %collective-permute-done.3.refs_1_, f32[896,128]{1,0:T(8,128)S(1)} %get-tuple-element.23.refs_2_, f32[896,256]{1,0:T(8,128)S(1)} %get-tuple-element.24.refs_3_), custom_call_target="tpu_custom_call" | custom-call | tf_op jit(solution)/shard_map/pallas_call | solution.py:130
  23.3 0.0 copy-done
  23.3 2.1 %convolution_convert_fusion = bf16[128,3584]{1,0:T(8,128)(2,1)} fusion(bf16[128,896]{1,0:T(8,128)(2,1)S(1)} %shard_map.51, bf16[896,3584]{1,0:T(8,128)(2,1)S(1)} %copy-done), kind=kOutput, calls=%fused_computation | convolution fusion | flops 822542336 | bytes 7569408 | tf_op jit(solution)/shard_map/dot_general | solution.py:140
  (3 shorter events, 0.0 us)
Async XLA Ops:
  0.0 23.3 %copy-start = (bf16[896,3584]{1,0:T(8,128)(2,1)S(1)}, bf16[896,3584]{1,0:T(8,128)(2,1)}, u32[]{:S(2)}) copy-start(bf16[896,3584]{1,0:T(8,128)(2,1)} %param.7) | copy-start | bytes 19267588
  1.0 7.8 %collective-permute-start = (bf16[128,256]{1,0:T(8,128)(2,1)S(1)}, bf16[128,256]{1,0:T(8,128)(2,1)S(1)}, u32[]{:S(2)}, u32[]{:S(2)}) collective-permute-start(bf16[128,256]{1,0:T(8,128)(2,1)S(1)} %shard_map.47.refs_1_), channel_id=1, source_target_pairs={{0,8},{1,9},{2,10},{3,11},{4,12},{5,13},{6,14},{7,15},{8,0},{9,1},... | collective-permute-start | bytes 196616 | tf_op jit(solution)/shard_map/ppermute | solution.py:170
  5.1 6.5 %collective-permute-start.1 = (bf16[128,256]{1,0:T(8,128)(2,1)S(1)}, bf16[128,256]{1,0:T(8,128)(2,1)S(1)}, u32[]{:S(2)}, u32[]{:S(2)}) collective-permute-start(bf16[128,256]{1,0:T(8,128)(2,1)S(1)} %shard_map.47.refs_1_), channel_id=1, source_target_pairs={{0,12},{1,13},{2,14},{3,15},{4,8},{5,9},{6,10},{7,11},{8,4},{9,5},... | collective-permute-start | bytes 196616 | tf_op jit(solution)/shard_map/ppermute | solution.py:170
  6.4 5.2 %collective-permute-start.4 = (bf16[128,256]{1,0:T(8,128)(2,1)S(1)}, bf16[128,256]{1,0:T(8,128)(2,1)S(1)}, u32[]{:S(2)}, u32[]{:S(2)}) collective-permute-start(bf16[128,256]{1,0:T(8,128)(2,1)S(1)} %shard_map.47.refs_1_), channel_id=1, source_target_pairs={{0,2},{1,3},{2,0},{3,1},{4,6},{5,7},{6,4},{7,5},{8,10},{9,11},{10,... | collective-permute-start | bytes 196616 | tf_op jit(solution)/shard_map/ppermute | solution.py:170
  8.0 4.3 %collective-permute-start.7 = (bf16[128,256]{1,0:T(8,128)(2,1)S(1)}, bf16[128,256]{1,0:T(8,128)(2,1)S(1)}, u32[]{:S(2)}, u32[]{:S(2)}) collective-permute-start(bf16[128,256]{1,0:T(8,128)(2,1)S(1)} %shard_map.47.refs_1_), channel_id=1, source_target_pairs={{0,4},{1,5},{2,6},{3,7},{4,0},{5,1},{6,2},{7,3},{8,12},{9,13},{10,... | collective-permute-start | bytes 196616 | tf_op jit(solution)/shard_map/ppermute | solution.py:170
  12.3 8.6 %collective-permute-start.8 = (bf16[512,256]{1,0:T(8,128)(2,1)S(1)}, bf16[512,256]{1,0:T(8,128)(2,1)S(1)}, u32[]{:S(2)}, u32[]{:S(2)}) collective-permute-start(bf16[512,256]{1,0:T(8,128)(2,1)S(1)} %pad_maximum_fusion), channel_id=1, source_target_pairs={{0,1},{1,0},{2,3},{3,2},{4,5},{5,4},{6,7},{7,6},{8,9},{9,8},{10,11... | collective-permute-start | bytes 786440 | tf_op jit(solution)/shard_map/ppermute | solution.py:170
  12.4 5.9 %collective-permute-start.2 = (bf16[256,256]{1,0:T(8,128)(2,1)S(1)}, bf16[256,256]{1,0:T(8,128)(2,1)S(1)}, u32[]{:S(2)}, u32[]{:S(2)}) collective-permute-start(bf16[256,256]{1,0:T(8,128)(2,1)S(1)} %constant_dynamic-update-slice_fusion), channel_id=1, source_target_pairs={{0,2},{1,3},{2,0},{3,1},{4,6},{5,7},{6,4},{7,5},{8,10},{9,11},{10,... | collective-permute-start | bytes 393224 | tf_op jit(solution)/shard_map/ppermute | solution.py:170
  13.6 5.2 %collective-permute-start.5 = (bf16[128,256]{1,0:T(8,128)(2,1)S(1)}, bf16[128,256]{1,0:T(8,128)(2,1)S(1)}, u32[]{:S(2)}, u32[]{:S(2)}) collective-permute-start(bf16[128,256]{1,0:T(8,128)(2,1)S(1)} %collective-permute-done.4.refs_3_), channel_id=1, source_target_pairs={{0,4},{1,5},{2,6},{3,7},{4,0},{5,1},{6,2},{7,3},{8,12},{9,13},{10,... | collective-permute-start | bytes 196616 | tf_op jit(solution)/shard_map/ppermute | solution.py:170
  18.3 4.4 %collective-permute-start.3 = (bf16[256,256]{1,0:T(8,128)(2,1)S(1)}, bf16[256,256]{1,0:T(8,128)(2,1)S(1)}, u32[]{:S(2)}, u32[]{:S(2)}) collective-permute-start(bf16[256,256]{1,0:T(8,128)(2,1)S(1)} %collective-permute-done.2.refs_2_), channel_id=1, source_target_pairs={{0,1},{1,0},{2,3},{3,2},{4,5},{5,4},{6,7},{7,6},{8,9},{9,8},{10,11... | collective-permute-start | bytes 393224 | tf_op jit(solution)/shard_map/ppermute | solution.py:170
  18.3 1.5 %collective-permute-start.9 = (bf16[128,256]{1,0:T(8,128)(2,1)S(1)}, bf16[128,256]{1,0:T(8,128)(2,1)S(1)}, u32[]{:S(2)}, u32[]{:S(2)}) collective-permute-start(bf16[128,256]{1,0:T(8,128)(2,1)S(1)} %shard_map.47.refs_1_), channel_id=1, source_target_pairs={{0,1},{1,0},{2,3},{3,2},{4,5},{5,4},{6,7},{7,6},{8,9},{9,8},{10,11... | collective-permute-start | bytes 196616 | tf_op jit(solution)/shard_map/ppermute | solution.py:170
  18.8 3.0 %collective-permute-start.6 = (bf16[128,256]{1,0:T(8,128)(2,1)S(1)}, bf16[128,256]{1,0:T(8,128)(2,1)S(1)}, u32[]{:S(2)}, u32[]{:S(2)}) collective-permute-start(bf16[128,256]{1,0:T(8,128)(2,1)S(1)} %collective-permute-done.5.refs_1_), channel_id=1, source_target_pairs={{0,1},{1,0},{2,3},{3,2},{4,5},{5,4},{6,7},{7,6},{8,9},{9,8},{10,11... | collective-permute-start | bytes 196616 | tf_op jit(solution)/shard_map/ppermute | solution.py:170
